TPU v7x, 256 devices: a whole 4x4x8 slice. The times are simulated.
256 devices in a mesh: row: 64 (over z, x, core), col: 4 (over y).
Axes of the slice: x: 4, y: 4, z: 8, core: 2. Of those that a mesh axis runs over, the one named last changes fastest.
Arguments:
- tile_values: bfloat16 [64, 4, 360, 128, 128], P('row', 'col')
- tile_places: int32 [64, 4, 2, 360], P('row', 'col'), may hold values from 0 to 383, as said below
- tile_counts: int32 [64, 4], P('row', 'col'), may hold values from 90 to 360, as said below
- sketch: bfloat16 [196608, 512], P('col'), may hold values from -6 to 6
Outputs:
- range_basis: float32 [196608, 512], P(('row', 'col'))
- triangle: float32 [512, 512], replicated
Inputs may be any that keep to these rules, and one draw needn't show every extreme that they name: `tile_places`: entry [r, c, 0, t] is the slot's tile row among the 24 tile rows of row block r and entry [r, c, 1, t] its tile column among the 384 tile columns of column block c; the 360 slots of one block pair name distinct positions, padded slots included. Slots t < tile_counts[r, c] hold the live tiles of block pair (r, c); later slots are padding and contribute nothing. Some block pair holds exactly 360 live tiles.
All inputs are finite; a program needn't handle non-finite values.
Results may differ from a plain program's by a relative error of at most 0.0003.
Values sent between devices are 32-bit elements; how exact they have to be, the bound alone decides.
A program may use at most 192 MiB of HBM per device.

v0:
```python
import math

import jax
import jax.numpy as jnp
from jax import lax
from jax.sharding import PartitionSpec as P


def swapped(block, axis, distance):
    count = lax.axis_size(axis)
    route = []
    for low in range(count):
        high = low | 1 << distance
        if high != low and high < count:
            route += [(low, high), (high, low)]
    return lax.ppermute(block, axis, route)


def add_tiles(
    tile_stack,
    panels,
    row_index,
    column_index,
    slot_order,
    first_pos,
    end_pos,
    row_base,
    out_rows,
    block_size,
):
    tile_size = tile_stack.shape[1]
    sketch_width = panels.shape[2]
    padded_order = jnp.concatenate([slot_order, jnp.zeros((block_size,), jnp.int32)])
    offsets = jnp.arange(block_size, dtype=jnp.int32)
    turn_count = jnp.maximum(end_pos - first_pos + block_size - 1, 0) // block_size

    def add_block(turn_index, partial_value):
        first_slot = first_pos + turn_index * block_size
        chosen = lax.dynamic_slice_in_dim(padded_order, first_slot, block_size, 0)
        live_mask = first_slot + offsets < end_pos
        picked = panels[column_index[chosen]]
        products = jnp.einsum(
            "tab,tbk->tak", tile_stack[chosen], picked, preferred_element_type=jnp.float32
        )
        products = jnp.where(live_mask[:, None, None], products, 0.0)
        targets = jnp.where(live_mask, row_index[chosen] - row_base, 0)
        return partial_value.at[targets].add(products)

    return lax.fori_loop(
        0, turn_count, add_block, jnp.zeros((out_rows, tile_size, sketch_width), jnp.float32)
    )


def across_rows(gram_part):
    for bit_index in range(lax.axis_size("row").bit_length() - 1):
        partner = swapped(gram_part, "row", bit_index)
        gram_part = gram_part + partner
    return gram_part


def across_cols(gram_part):
    for bit_index in range(lax.axis_size("col").bit_length() - 1):
        partner = swapped(gram_part, "col", bit_index)
        gram_part = gram_part + partner
    return gram_part


def body(tile_values, tile_places, tile_counts, sketch):
    tile_stack = tile_values[0, 0]
    slot_count = tile_stack.shape[0]
    tile_size = tile_stack.shape[1]
    sketch_width = sketch.shape[1]
    row_devices = lax.axis_size("row")
    col_devices = lax.axis_size("col")
    local_rows = sketch.shape[0] // row_devices
    tile_rows = local_rows * col_devices // tile_size
    panels = sketch.reshape(-1, tile_size, sketch_width)
    row_index = tile_places[0, 0, 0]
    column_index = tile_places[0, 0, 1]
    live_count = tile_counts[0, 0]
    block_size = math.gcd(slot_count, 40)
    slot_ids = jnp.arange(slot_count, dtype=jnp.int32)
    partial_value = add_tiles(
        tile_stack,
        panels,
        row_index,
        column_index,
        slot_ids,
        0,
        live_count,
        0,
        tile_rows,
        block_size,
    )
    own_rows = lax.psum_scatter(
        partial_value.reshape(tile_rows * tile_size, sketch_width),
        "col",
        scatter_dimension=0,
        tiled=True,
    )
    gram_local = jnp.dot(
        own_rows.T, own_rows, precision=lax.Precision.HIGHEST, preferred_element_type=jnp.float32
    )
    gram_whole = across_cols(across_rows(gram_local))
    chol_lower = jnp.linalg.cholesky(gram_whole)
    order_scale = math.sqrt(local_rows * row_devices * col_devices)
    basis_rows = (
        jax.scipy.linalg.solve_triangular(chol_lower, own_rows.T, lower=True).T * order_scale
    )
    return (basis_rows, chol_lower.T / order_scale)


def solution(mesh):
    in_specs = (
        P("row", "col", None, None, None),
        P("row", "col", None, None),
        P("row", "col"),
        P("col", None),
    )
    out_specs = (P(("row", "col"), None), P())
    return jax.shard_map(body, mesh=mesh, in_specs=in_specs, out_specs=out_specs, check_vma=False)
```

profile of v0, /device:TPU:1, one launch (start us, length us, event | category | flops | bytes accessed | tf_op | source)
XLA Modules:
  0.0 898.0 jit_solution(1960316329361594252)
XLA Ops:
  12.1 237.5 %while.14 = (s32[]{:T(128)}, f32[24,128,512]{2,1,0:T(8,128)}, s32[]{:T(128)}, s32[]{:T(128)}, s32[360]{0:T(512)S(1)}, /*index=5*/bf16[360,128,128]{2,1,0:T(8,128...) while((s32[]{:T(128)}, f32[24,128,512]{2,1,0:T(8,128)}, ...), condition=%wide.region_2.3_spmd.clone, body=%wide.region_0.2_spmd.clone.sunk | while | flops 676334080 | bytes 61615024 | solution.py:49
  36.4 22.9 %scatter_fusion = f32[24,128,512]{2,1,0:T(8,128)} fusion(f32[24,128,512]{2,1,0:T(8,128)} %get-tuple-element.258, s32[40]{0:T(128)S(1)} %get-tuple-element.242, f32[40,128,512]{2,1,0:T(8,128)} %broadcast_select_fusion.2), kind=kCustom, calls=%fused_computation.4.clone.clone.1 | custom fusion | flops 2621440 | bytes 31457440 | tf_op jit(solution)/shard_map/while/body/scatter-add | solution.py:47
  83.8 23.1 %scatter_fusion = f32[24,128,512]{2,1,0:T(8,128)} fusion(f32[24,128,512]{2,1,0:T(8,128)} %get-tuple-element.258, s32[40]{0:T(128)S(1)} %get-tuple-element.242, f32[40,128,512]{2,1,0:T(8,128)} %broadcast_select_fusion.2), kind=kCustom, calls=%fused_computation.4.clone.clone.1 | custom fusion | flops 2621440 | bytes 31457440 | tf_op jit(solution)/shard_map/while/body/scatter-add | solution.py:47
  131.3 23.1 %scatter_fusion = f32[24,128,512]{2,1,0:T(8,128)} fusion(f32[24,128,512]{2,1,0:T(8,128)} %get-tuple-element.258, s32[40]{0:T(128)S(1)} %get-tuple-element.242, f32[40,128,512]{2,1,0:T(8,128)} %broadcast_select_fusion.2), kind=kCustom, calls=%fused_computation.4.clone.clone.1 | custom fusion | flops 2621440 | bytes 31457440 | tf_op jit(solution)/shard_map/while/body/scatter-add | solution.py:47
  179.0 23.1 %scatter_fusion = f32[24,128,512]{2,1,0:T(8,128)} fusion(f32[24,128,512]{2,1,0:T(8,128)} %get-tuple-element.258, s32[40]{0:T(128)S(1)} %get-tuple-element.242, f32[40,128,512]{2,1,0:T(8,128)} %broadcast_select_fusion.2), kind=kCustom, calls=%fused_computation.4.clone.clone.1 | custom fusion | flops 2621440 | bytes 31457440 | tf_op jit(solution)/shard_map/while/body/scatter-add | solution.py:47
  210.3 8.5 gather_fusion.3
  226.7 22.9 %scatter_fusion = f32[24,128,512]{2,1,0:T(8,128)} fusion(f32[24,128,512]{2,1,0:T(8,128)} %get-tuple-element.258, s32[40]{0:T(128)S(1)} %get-tuple-element.242, f32[40,128,512]{2,1,0:T(8,128)} %broadcast_select_fusion.2), kind=kCustom, calls=%fused_computation.4.clone.clone.1 | custom fusion | flops 2621440 | bytes 31457440 | tf_op jit(solution)/shard_map/while/body/scatter-add | solution.py:47
  249.6 258.8 %reduce-scatter.2.cloned.1.call-done = f32[768,512]{1,0:T(8,128)} async-done(((f32[3072,512]{1,0:T(8,128)}), f32[768,512]{1,0:T(8,128)}) %reduce-scatter.2.cloned.1.call-update) | async-done | bytes 1572880 | tf_op jit(solution)/shard_map/reduce_scatter | solution.py:95
  517.6 23.2 %collective-permute-done.1 = f32[512,512]{0,1:T(8,128)S(1)} collective-permute-done((f32[512,512]{0,1:T(8,128)S(1)}, f32[512,512]{0,1:T(8,128)S(1)}, u32[]{:S(2)}, u32[]{:S(2)}) %collective-permute-start.1) | collective-permute-done | bytes 1048608 | tf_op jit(solution)/shard_map/ppermute | solution.py:16
  543.8 22.3 %collective-permute-done.2 = f32[512,512]{0,1:T(8,128)S(1)} collective-permute-done((f32[512,512]{0,1:T(8,128)S(1)}, f32[512,512]{0,1:T(8,128)S(1)}, u32[]{:S(2)}, u32[]{:S(2)}) %collective-permute-start.2) | collective-permute-done | bytes 1048608 | tf_op jit(solution)/shard_map/ppermute | solution.py:16
  567.6 21.4 %collective-permute-done.3 = f32[512,512]{0,1:T(8,128)S(1)} collective-permute-done((f32[512,512]{0,1:T(8,128)S(1)}, f32[512,512]{0,1:T(8,128)S(1)}, u32[]{:S(2)}, u32[]{:S(2)}) %collective-permute-start.3) | collective-permute-done | bytes 1048608 | tf_op jit(solution)/shard_map/ppermute | solution.py:16
  591.5 45.2 %collective-permute-done.4 = f32[512,512]{0,1:T(8,128)S(1)} collective-permute-done((f32[512,512]{0,1:T(8,128)S(1)}, f32[512,512]{0,1:T(8,128)S(1)}, u32[]{:S(2)}, u32[]{:S(2)}) %collective-permute-start.4) | collective-permute-done | bytes 1048608 | tf_op jit(solution)/shard_map/ppermute | solution.py:16
  643.4 45.6 %collective-permute-done.5 = f32[512,512]{0,1:T(8,128)S(1)} collective-permute-done((f32[512,512]{0,1:T(8,128)S(1)}, f32[512,512]{0,1:T(8,128)S(1)}, u32[]{:S(2)}, u32[]{:S(2)}) %collective-permute-start.5) | collective-permute-done | bytes 1048608 | tf_op jit(solution)/shard_map/ppermute | solution.py:16
  689.3 23.3 %collective-permute-done.6 = f32[512,512]{0,1:T(8,128)S(1)} collective-permute-done((f32[512,512]{0,1:T(8,128)S(1)}, f32[512,512]{0,1:T(8,128)S(1)}, u32[]{:S(2)}, u32[]{:S(2)}) %collective-permute-start.6) | collective-permute-done | bytes 1048608 | tf_op jit(solution)/shard_map/ppermute | solution.py:16
  714.3 22.7 %collective-permute-done.7 = f32[512,512]{0,1:T(8,128)S(1)} collective-permute-done((f32[512,512]{0,1:T(8,128)S(1)}, f32[512,512]{0,1:T(8,128)S(1)}, u32[]{:S(2)}, u32[]{:S(2)}) %collective-permute-start.7) | collective-permute-done | bytes 1048608 | tf_op jit(solution)/shard_map/ppermute | solution.py:16
  738.8 11.7 %cholesky.104 = f32[128,128]{1,0:T(8,128)S(1)} custom-call(f32[128,128]{1,0:T(8,128)S(1)} %cholesky.266), custom_call_target="Cholesky" | custom-call | tf_op jit(solution)/shard_map/jit(cholesky)/cholesky | solution.py:105
  750.7 9.8 %custom-call.31 = f32[1,128,128]{1,2,0:T(8,128)S(1)} custom-call(f32[1,128,128]{2,1,0:T(8,128)S(1)} %get-tuple-element.156), custom_call_target="InvertDiagBlocksLowerTriangular" | custom-call | tf_op jit(solution)/shard_map/jit(cholesky)/cholesky | solution.py:105
  763.0 11.7 %cholesky.217 = f32[128,128]{1,0:T(8,128)S(1)} custom-call(f32[128,128]{1,0:T(8,128)S(1)} %cholesky.270), custom_call_target="Cholesky" | custom-call | tf_op jit(solution)/shard_map/jit(cholesky)/cholesky | solution.py:105
  774.8 10.0 %custom-call.32 = f32[1,128,128]{1,2,0:T(8,128)S(1)} custom-call(f32[1,128,128]{2,1,0:T(8,128)S(1)} %get-tuple-element.153), custom_call_target="InvertDiagBlocksLowerTriangular" | custom-call | tf_op jit(solution)/shard_map/jit(cholesky)/cholesky | solution.py:105
  786.4 11.7 %cholesky.238 = f32[128,128]{1,0:T(8,128)S(1)} custom-call(f32[128,128]{1,0:T(8,128)S(1)} %cholesky.275), custom_call_target="Cholesky" | custom-call | tf_op jit(solution)/shard_map/jit(cholesky)/cholesky | solution.py:105
  798.1 9.8 %custom-call.33 = f32[1,128,128]{1,2,0:T(8,128)S(1)} custom-call(f32[1,128,128]{2,1,0:T(8,128)S(1)} %get-tuple-element.150), custom_call_target="InvertDiagBlocksLowerTriangular" | custom-call | tf_op jit(solution)/shard_map/jit(cholesky)/cholesky | solution.py:105
  809.4 11.7 %cholesky.255 = f32[128,128]{1,0:T(8,128)S(1)} custom-call(f32[128,128]{1,0:T(8,128)S(1)} %slice_subtract_fusion.2), custom_call_target="Cholesky" | custom-call | tf_op jit(solution)/shard_map/jit(cholesky)/cholesky | solution.py:105
  827.5 11.6 %while.13 = (s32[]{:T(128)}, f32[512,512]{1,0:T(8,128)}, s32[4,2]{0,1:T(2,128)S(1)}, f32[4,128,128]{2,1,0:T(8,128)S(1)}, s32[]{:T(128)}) while((s32[]{:T(128)}, f32[512,512]{1,0:T(8,128)}, s32[4,2]{0,1:T(2,128)S(1)}, f32[4,128,128]{2,1,0:T(8,128)S(1)}, s32[]{:T(128)}) %tuple.61), condition=%wide.while_cond, body=%wide.while_body.sunk | while | flops 2 | bytes 131189 | solution.py:108
  839.1 39.3 %custom-call.34 = f32[4,128,128]{1,2,0:T(8,128)S(1)} custom-call(f32[4,128,128]{2,1,0:T(8,128)S(1)} %get-tuple-element.91), custom_call_target="InvertDiagBlocksLowerTriangular" | custom-call | tf_op jit(solution)/shard_map/jit(_solve_triangular)/triangular_solve | solution.py:108
  (122 shorter events, 178.3 us)
Async XLA Ops:
  7.2 501.2 %reduce-scatter.2.cloned.1.call-start = ((), (), s32[]{:S(2)}) async-start(), calls=%async_computation.1 | async-start | bytes 7864320 | tf_op jit(solution)/shard_map/reduce_scatter | solution.py:95
  513.0 3.1 collective-permute-start
  516.3 24.4 %collective-permute-start.1 = (f32[512,512]{0,1:T(8,128)S(1)}, f32[512,512]{0,1:T(8,128)S(1)}, u32[]{:S(2)}, u32[]{:S(2)}) collective-permute-start(f32[512,512]{0,1:T(8,128)S(1)} %add.137), channel_id=1, source_target_pairs={{0,8},{8,0},{4,12},{12,4},{16,24},{24,16},{20,28},{28,20},{32,40},... | collective-permute-start | bytes 3145736 | tf_op jit(solution)/shard_map/ppermute | solution.py:16
  541.0 25.1 %collective-permute-start.2 = (f32[512,512]{0,1:T(8,128)S(1)}, f32[512,512]{0,1:T(8,128)S(1)}, u32[]{:S(2)}, u32[]{:S(2)}) collective-permute-start(f32[512,512]{0,1:T(8,128)S(1)} %add.138), channel_id=1, source_target_pairs={{0,16},{16,0},{4,20},{20,4},{8,24},{24,8},{12,28},{28,12},{32,48},... | collective-permute-start | bytes 3145736 | tf_op jit(solution)/shard_map/ppermute | solution.py:16
  566.3 22.7 %collective-permute-start.3 = (f32[512,512]{0,1:T(8,128)S(1)}, f32[512,512]{0,1:T(8,128)S(1)}, u32[]{:S(2)}, u32[]{:S(2)}) collective-permute-start(f32[512,512]{0,1:T(8,128)S(1)} %add.139), channel_id=1, source_target_pairs={{0,32},{32,0},{4,36},{36,4},{8,40},{40,8},{12,44},{44,12},{16,48},... | collective-permute-start | bytes 3145736 | tf_op jit(solution)/shard_map/ppermute | solution.py:16
  589.2 47.5 %collective-permute-start.4 = (f32[512,512]{0,1:T(8,128)S(1)}, f32[512,512]{0,1:T(8,128)S(1)}, u32[]{:S(2)}, u32[]{:S(2)}) collective-permute-start(f32[512,512]{0,1:T(8,128)S(1)} %add.140), channel_id=1, source_target_pairs={{0,64},{64,0},{4,68},{68,4},{8,72},{72,8},{12,76},{76,12},{16,80},... | collective-permute-start | bytes 3145736 | tf_op jit(solution)/shard_map/ppermute | solution.py:16
  636.9 52.1 %collective-permute-start.5 = (f32[512,512]{0,1:T(8,128)S(1)}, f32[512,512]{0,1:T(8,128)S(1)}, u32[]{:S(2)}, u32[]{:S(2)}) collective-permute-start(f32[512,512]{0,1:T(8,128)S(1)} %add.141), channel_id=1, source_target_pairs={{0,128},{128,0},{4,132},{132,4},{8,136},{136,8},{12,140},{140,12},... | collective-permute-start | bytes 3145736 | tf_op jit(solution)/shard_map/ppermute | solution.py:16
  689.2 23.4 %collective-permute-start.6 = (f32[512,512]{0,1:T(8,128)S(1)}, f32[512,512]{0,1:T(8,128)S(1)}, u32[]{:S(2)}, u32[]{:S(2)}) collective-permute-start(f32[512,512]{0,1:T(8,128)S(1)} %add.142), channel_id=1, source_target_pairs={{0,1},{1,0},{2,3},{3,2},{4,5},{5,4},{6,7},{7,6},{8,9},{9,8},{10,11... | collective-permute-start | bytes 3145736 | tf_op jit(solution)/shard_map/ppermute | solution.py:16
  712.8 24.2 %collective-permute-start.7 = (f32[512,512]{0,1:T(8,128)S(1)}, f32[512,512]{0,1:T(8,128)S(1)}, u32[]{:S(2)}, u32[]{:S(2)}) collective-permute-start(f32[512,512]{0,1:T(8,128)S(1)} %add.143), channel_id=1, source_target_pairs={{0,2},{2,0},{1,3},{3,1},{4,6},{6,4},{5,7},{7,5},{8,10},{10,8},{9,1... | collective-permute-start | bytes 3145736 | tf_op jit(solution)/shard_map/ppermute | solution.py:16
  737.8 1.0 copy-start.2
  825.9 52.5 %copy-start = (f32[768,512]{1,0:T(8,128)S(1)}, f32[768,512]{1,0:T(8,128)}, u32[]{:S(2)}) copy-start(f32[768,512]{1,0:T(8,128)} %reduce-scatter.2.cloned.1.call-done) | copy-start | bytes 4718596
  887.8 1.6 copy-start.1
Sparse Core Ops, SparseCore 0:
  249.7 258.6 reduce-scatter.1
where the time goes:
time: 911 us; the launch traced here: 898 us
  waiting for transfers between devices  465 us (51%)
  other arithmetic  244 us (27%)
  local copies, waits for them, and re-layouts  95.5 us (10%)
  matrix products  59.1 us (6%)
  between operations  18 us (2%)
  starting transfers between devices  16.7 us (2%)
    reduce_scatter x1, waiting for transfers between devices, body(): lax.psum_scatter(partial_value.reshape(tile_rows * tile_size, sketch_widt...  259 us
    ppermute x8, waiting for transfers between devices, swapped(): return lax.ppermute(block, axis, route)  206 us
    scatter-add x5, other arithmetic, add_block(): return partial_value.at[targets].add(products)  115 us
    another operation x14, other arithmetic, body(): chol_lower = jnp.linalg.cholesky(gram_whole)  78.9 us
    gather x10, local copies, waits for them, and re-layouts, add_block(): picked = panels[column_index[chosen]]  45.7 us
    dot_general x5, matrix products, add_block(): jnp.einsum('tab,tbk->tak', tile_stack[chosen], picked, preferred_element_...  39.9 us
    another operation x2, other arithmetic, body(): jax.scipy.linalg.solve_triangular(chol_lower, own_rows.T, lower=True)  39.3 us
    gather x5, local copies, waits for them, and re-layouts, add_block(): tile_stack[chosen]  25.8 us
  transfers between devices with their start and end apart: 9, of which 9 were waited for; matrix products, arithmetic and copies ran while one was open for 0% of the time, Pallas kernels for 0%

commit v1 on v0

v1 whole, which is shorter than its diff:
```python
import functools, math
import jax
import jax.numpy as jnp
from jax import lax
from jax.experimental import pallas as pl
from jax.experimental.pallas import tpu as pltpu
from jax.sharding import PartitionSpec as P

GROUP = 4
TURN = 3
RING = 12

def sparse_kernel(base, plan_ref, span_ref, tiles, panels, *rest):
    nout = len(rest) - 6
    outs = rest[:nout]
    lhs, rhs, sums, tsem, psem, osem = rest[nout:]
    first = span_ref[0]
    last = span_ref[1]
    size = tiles.shape[1]
    rows_each = outs[0].shape[0]
    spare = nout * rows_each

    def parts(g, k):
        word = plan_ref[g * GROUP + k]
        s = lax.rem(g, RING)
        live = word >= (1 << 23)
        tile = pltpu.make_async_copy(tiles.at[word & 511], lhs.at[s, :, pl.ds(k * size, size)], tsem.at[s, k])
        panel = pltpu.make_async_copy(panels.at[(word >> 9) & 511], rhs.at[s, pl.ds(k * size, size), :], psem.at[s, k])
        return live, tile, panel, s

    def issue(g):
        for k in range(GROUP):
            live, tile, panel, s = parts(g, k)
            @pl.when(live)
            def _():
                tile.start()
                panel.start()
            if k:
                @pl.when(jnp.logical_not(live))
                def _():
                    lhs[s, :, k * size:(k + 1) * size] = jnp.zeros((size, size), lhs.dtype)
                    rhs[s, k * size:(k + 1) * size, :] = jnp.zeros((size, rhs.shape[2]), rhs.dtype)

    def prime(g, c):
        issue(g)
        return c

    lax.fori_loop(first, jnp.minimum(first + RING - TURN, last), prime, 0)

    def clear(i, c):
        sums[i] = jnp.zeros(sums.shape[1:], sums.dtype)
        return c

    lax.fori_loop(0, sums.shape[0], clear, 0)

    def step(turn, carry):
        g0 = first + turn * TURN
        for u in range(TURN):
            g = g0 + u
            @pl.when(g + RING - TURN < last)
            def _():
                issue(g + RING - TURN)
            @pl.when(g < last)
            def _():
                for k in range(GROUP):
                    live, tile, panel, s = parts(g, k)
                    @pl.when(live)
                    def _():
                        tile.wait()
                        panel.wait()
        for u in range(TURN):
            g = g0 + u
            s = lax.rem(g, RING)
            place = jnp.where(g < last, ((plan_ref[jnp.minimum(g, last - 1) * GROUP] >> 18) & 31) - base, spare)
            prod = jnp.dot(lhs[s], rhs[s], preferred_element_type=jnp.float32)
            sums[place] = sums[place] + prod
        return carry

    lax.fori_loop(0, lax.div(last - first + TURN - 1, TURN), step, 0)
    copies = [pltpu.make_async_copy(sums.at[pl.ds(i * rows_each, rows_each)], o, osem.at[i]) for i, o in enumerate(outs)]
    for c in copies:
        c.start()
    for c in copies:
        c.wait()

def sparse_sum(plan, span, tiles, panels, base, shape):
    nout, rows = shape
    width = panels.shape[2]
    size = tiles.shape[1]
    return pl.pallas_call(
        functools.partial(sparse_kernel, base),
        grid_spec=pltpu.PrefetchScalarGridSpec(
            num_scalar_prefetch=2, grid=(),
            in_specs=[pl.BlockSpec(memory_space=pl.ANY)] * 2,
            out_specs=[pl.BlockSpec(memory_space=pl.ANY)] * nout,
            scratch_shapes=[pltpu.VMEM((RING, size, GROUP * size), tiles.dtype), pltpu.VMEM((RING, GROUP * size, width), panels.dtype),
                            pltpu.VMEM((nout * rows + 1, size, width), jnp.float32),
                            pltpu.SemaphoreType.DMA((RING, GROUP)), pltpu.SemaphoreType.DMA((RING, GROUP)), pltpu.SemaphoreType.DMA((nout,))]),
        out_shape=[jax.ShapeDtypeStruct((rows, size, width), jnp.float32)] * nout,
        compiler_params=pltpu.CompilerParams(vmem_limit_bytes=40 << 20),
        cost_estimate=pl.CostEstimate(flops=2 * 360 * 128 * 128 * 512 * rows * nout // 24, bytes_accessed=50_000_000 * rows * nout // 24, transcendentals=0),
        name="tile_sums",
    )(plan, span, tiles, panels)

def make_plan(places, count, me, ncol, chunk_rows):
    rows = places[0]
    cols = places[1]
    n = rows.shape[0]
    nplace = ncol * chunk_rows
    ids = jnp.arange(n, dtype=jnp.int32)
    half = chunk_rows // 2
    dest = rows // chunk_rows
    sub = rows % chunk_rows
    step = jnp.where(sub < half, (me - 1 - dest) % ncol, (dest - 1 - me) % ncol)
    live = ids < count
    place = jnp.where(live, step * chunk_rows + sub, nplace)
    rank = jnp.sum(((place[None, :] == place[:, None]) & (ids[None, :] < ids[:, None])).astype(jnp.int32), axis=1)
    which = jnp.arange(nplace, dtype=jnp.int32)
    held = jnp.sum((place[None, :] == which[:, None]).astype(jnp.int32), axis=1)
    groups = (held + GROUP - 1) // GROUP
    ahead = jnp.sum(jnp.where(which[None, :] < place[:, None], groups[None, :], 0), axis=1)
    spot = jnp.where(live, ahead * GROUP + rank, -1)
    word = ids | (cols << 9) | (place << 18) | (1 << 23)
    total = -(-(n // GROUP + nplace) * GROUP // 128) * 128
    plan = jnp.sum(jnp.where(spot[None, :] == jnp.arange(total, dtype=jnp.int32)[:, None], word[None, :], 0), axis=1)
    n0 = jnp.sum(jnp.where(which < chunk_rows, groups, 0))
    n1 = jnp.sum(groups)
    return plan, jnp.stack([jnp.int32(0), n0]), jnp.stack([n0, n1])


HI = lax.Precision.HIGHEST

def dot_hi(a, b, dims):
    return lax.dot_general(a, b, (dims, ((), ())), precision=HI, preferred_element_type=jnp.float32)

def factor_block(a_ref, w_ref, u_ref, m):
    n = 128
    nv = n // 8
    lane = lax.broadcasted_iota(jnp.int32, (8, n), 1)
    sub = lax.broadcasted_iota(jnp.int32, (8, n), 0)
    a = [a_ref[8 * v:8 * v + 8, :] for v in range(nv)]
    b = [jnp.where(lane == sub + 8 * v, 1.0, 0.0).astype(jnp.float32) for v in range(nv)]
    for r in range(nv):
        col = {}
        for v in range(r, nv):
            for k in range(8):
                col[k, v] = jnp.broadcast_to(a[v][:, 8 * r + k:8 * r + k + 1], (8, n))
        e = {}
        for k in range(8):
            for j in range(k, 8):
                e[k, j] = jnp.broadcast_to(col[j, r][k:k + 1, :], (8, n))
        ra = [jnp.broadcast_to(a[r][k:k + 1, :], (8, n)) for k in range(8)]
        rb = [jnp.broadcast_to(b[r][k:k + 1, :], (8, n)) for k in range(8)]
        for k in range(8):
            rs = lax.rsqrt(e[k, k])
            for j in range(k + 1, 8):
                e[k, j] = e[k, j] * rs
            for i in range(k + 1, 8):
                for j in range(i, 8):
                    e[i, j] = e[i, j] - e[k, i] * e[k, j]
            ra[k] = ra[k] * rs
            rb[k] = rb[k] * rs
            for j in range(k + 1, 8):
                ra[j] = ra[j] - e[k, j] * ra[k]
                rb[j] = rb[j] - e[k, j] * rb[k]
            for v in range(r + 1, nv):
                col[k, v] = col[k, v] * rs
                for j in range(k + 1, 8):
                    col[j, v] = col[j, v] - e[k, j] * col[k, v]
                a[v] = a[v] - col[k, v] * ra[k]
                b[v] = b[v] - col[k, v] * rb[k]
        ua, ub = ra[0], rb[0]
        for k in range(1, 8):
            ua = jnp.where(sub == k, ra[k], ua)
            ub = jnp.where(sub == k, rb[k], ub)
        u_ref[8 * r:8 * r + 8, :] = jnp.where(lane >= sub + 8 * r, ua, 0.0)
        w_ref[8 * r:8 * r + 8, :] = ub

def chol_kernel(scale, g_ref, s_ref, x_ref, t_ref, gw, xs, d_ref, w_ref, u_ref):
    n = g_ref.shape[0]
    nb = n // 128
    gw[...] = g_ref[...]
    xs[...] = s_ref[...] * scale
    t_ref[...] = jnp.zeros_like(t_ref)
    for k in range(nb):
        lo = 128 * k
        hi = lo + 128
        d_ref[...] = gw[lo:hi, lo:hi]
        factor_block(d_ref, w_ref, u_ref, k)
        w = w_ref[...]
        t_ref[lo:hi, lo:hi] = u_ref[...] * (1.0 / scale)
        xk = dot_hi(xs[:, lo:hi], w, ((1,), (1,)))
        x_ref[:, lo:hi] = xk
        if hi < n:
            up = dot_hi(w, gw[lo:hi, hi:n], ((1,), (0,)))
            t_ref[lo:hi, hi:n] = up * (1.0 / scale)
            gw[hi:n, hi:n] = gw[hi:n, hi:n] - dot_hi(up, up, ((0,), (0,)))
            xs[:, hi:n] = xs[:, hi:n] - dot_hi(xk, up, ((1,), (0,)))

def chol_solve(gram, rows, scale):
    m, n = rows.shape
    return pl.pallas_call(
        functools.partial(chol_kernel, scale),
        out_shape=(jax.ShapeDtypeStruct((m, n), jnp.float32), jax.ShapeDtypeStruct((n, n), jnp.float32)),
        in_specs=[pl.BlockSpec(memory_space=pltpu.VMEM)] * 2,
        out_specs=(pl.BlockSpec(memory_space=pltpu.VMEM),) * 2,
        scratch_shapes=[pltpu.VMEM((n, n), jnp.float32), pltpu.VMEM((m, n), jnp.float32),
                        pltpu.VMEM((128, 128), jnp.float32), pltpu.VMEM((128, 128), jnp.float32),
                        pltpu.VMEM((128, 128), jnp.float32)],
        name="factor_solve",
    )(gram, rows)


def shifted(block, distance):
    count = lax.axis_size("col")
    return lax.ppermute(block, "col", [(i, (i + distance) % count) for i in range(count)])


def body(tile_values, tile_places, tile_counts, sketch):
    tile_stack = tile_values[0, 0]
    tile_size = tile_stack.shape[1]
    sketch_width = sketch.shape[1]
    row_devices = lax.axis_size("row")
    col_devices = lax.axis_size("col")
    local_rows = sketch.shape[0] // row_devices
    chunk_rows = local_rows // tile_size
    half = chunk_rows // 2
    panels = sketch.reshape(-1, tile_size, sketch_width)
    me = lax.axis_index("col")
    plan, span0, span1 = make_plan(tile_places[0, 0], tile_counts[0, 0], me, col_devices, chunk_rows)
    up, down = sparse_sum(plan, span0, tile_stack, panels, 0, (2, half))
    later = sparse_sum(plan, span1, tile_stack, panels, chunk_rows, (2 * (col_devices - 1), half))
    for turn in range(col_devices - 1):
        up = shifted(up, 1) + later[2 * turn]
        down = shifted(down, -1) + later[2 * turn + 1]
    own_rows = jnp.concatenate([up, down], axis=0).reshape(local_rows, sketch_width)
    gram_local = jnp.dot(own_rows.T, own_rows, precision=HI, preferred_element_type=jnp.float32)
    gram_whole = lax.psum(gram_local, ("row", "col"))
    order_scale = math.sqrt(local_rows * row_devices * col_devices)
    basis_rows, upper = chol_solve(gram_whole, own_rows, order_scale)
    return basis_rows, upper


def solution(mesh):
    in_specs = (
        P("row", "col", None, None, None),
        P("row", "col", None, None),
        P("row", "col"),
        P("col", None),
    )
    out_specs = (P(("row", "col"), None), P())
    return jax.shard_map(body, mesh=mesh, in_specs=in_specs, out_specs=out_specs, check_vma=False)
```

time: 911 us -> 383 us (0.42); the launches traced: 898 us -> 383 us
  other arithmetic: 244 us -> 6.4 us
  waiting for transfers between devices: 465 us -> 302 us
  local copies, waits for them, and re-layouts: 95.5 us -> 4.35 us
  matrix products: 59.1 us -> 3.67 us
  Pallas kernels: 0 us -> 40 us
    psum x0 -> x1, waiting for transfers between devices: none -> 262 us  [body(): gram_whole = lax.psum(gram_local, ('row', 'col'))]
    reduce_scatter x1 -> x0, waiting for transfers between devices: 259 us -> none  [body(): lax.psum_scatter(partial_value.reshape(tile_rows * tile_size, sketch_widt...]
    ppermute x8 -> x6, waiting for transfers between devices: 206 us -> 40.5 us  [shifted(): lax.ppermute(block, 'col', [(i, (i + distance) % count) for i in range(co...]
    another operation x16 -> x1, other arithmetic: 118 us -> 1.41 us  [make_plan(): return (plan, jnp.stack([jnp.int32(0), n0]), jnp.stack([n0, n1]))]
    scatter-add x5 -> x0, other arithmetic: 115 us -> none  [add_block(): return partial_value.at[targets].add(products)]
    gather x20 -> x0, local copies, waits for them, and re-layouts: 75.4 us -> none  [the longest x10 45.7 us: add_block(): picked = panels[column_index[chosen]]]
    dot_general x6 -> x1, matrix products: 44.5 us -> 3.67 us  [body(): jnp.dot(own_rows.T, own_rows, precision=HI, preferred_element_type=jnp.fl...]
    pallas_call x0 -> x3, Pallas kernels: none -> 40 us  [the longest x1 26.3 us: chol_solve(): pl.pallas_call(functools.partial(chol_kernel, scale), out_shape=(jax.Shap...]
  transfers between devices with their start and end apart: 9 -> 7, of which waited for: 9 -> 4; matrix products, arithmetic and copies ran while one was open for 0% -> 1% of each run, Pallas kernels for 0% -> 2%
where the time goes in v1:
time: 383 us
  waiting for transfers between devices  302 us (79%)
  Pallas kernels  40 us (10%)
  between operations  14.8 us (4%)
  starting transfers between devices  11.8 us (3%)
  other arithmetic  6.4 us (2%)
  local copies, waits for them, and re-layouts  4.35 us (1%)
    psum x1, waiting for transfers between devices, body(): gram_whole = lax.psum(gram_local, ('row', 'col'))  262 us
    ppermute x6, waiting for transfers between devices, shifted(): lax.ppermute(block, 'col', [(i, (i + distance) % count) for i in range(co...  40.5 us
    pallas_call x1, Pallas kernels, chol_solve(): pl.pallas_call(functools.partial(chol_kernel, scale), out_shape=(jax.Shap...  26.3 us
    pallas_call x2, Pallas kernels, sparse_sum(): pl.pallas_call(functools.partial(sparse_kernel, base), grid_spec=pltpu.Pr...  13.7 us
    ppermute x6, starting transfers between devices, shifted(): lax.ppermute(block, 'col', [(i, (i + distance) % count) for i in range(co...  11.8 us
  transfers between devices with their start and end apart: 7, of which 4 were waited for; matrix products, arithmetic and copies ran while one was open for 1% of the time, Pallas kernels for 2%

profile of v1, /device:TPU:1, one launch (start us, length us, event | category | flops | bytes accessed | tf_op | source)
XLA Modules:
  0.0 383.3 jit_solution(15750768227382186493)
XLA Ops:
  7.2 0.7 compare_reduce_fusion
  7.9 0.8 shift-left_reduce_fusion
  9.5 0.2 convert_reduce_fusion
  9.7 0.7 fusion.8
  10.6 0.2 select_reduce_fusion.plan_ref
  10.7 1.4 pad_add_fusion
  12.1 4.4 %copy-done = bf16[1,1,360,128,128]{4,3,2,1,0:T(8,128)(2,1)S(1)} copy-done((bf16[1,1,360,128,128]{4,3,2,1,0:T(8,128)(2,1)S(1)}, bf16[1,1,360,128,128]{4,3,2,1,0:T(8,128)(2,1)}, u32[]{:S(2)}) %copy-start) | copy-done | bytes 11796504
  16.5 4.8 %tile_sums.2 = (f32[3,128,512]{2,1,0:T(8,128)S(1)}, f32[3,128,512]{2,1,0:T(8,128)S(1)}) custom-call(s32[512]{0:T(512)S(1)} %select_reduce_fusion.plan_ref, s32[2]{0:T(128)S(1)} %get-tuple-element.26.span_ref, bf16[360,128,128]{2,1,0:T(8,128)(2,1)S(1)} %bitcast.11, bf16[384,128,512]{2,1,0:T(8,128)(2,1)} %bitcast.12), custom_call_target="tpu_custom_call" | custom-call | flops 1509949440 | bytes 12500000 | tf_op jit(solution)/shard_map/tile_sums/pallas_call | solution.py:90
  21.3 2.3 collective-permute-start
  23.6 3.7 collective-permute-start.3
  27.3 8.9 %tile_sums.3 = (f32[3,128,512]{2,1,0:T(8,128)S(1)}, f32[3,128,512]{2,1,0:T(8,128)S(1)}, f32[3,128,512]{2,1,0:T(8,128)S(1)}, f32[3,128,512]{2,1,0:T(8,128)S(1)}, ...) custom-call(s32[512]{0:T(512)S(1)} %select_reduce_fusion.plan_ref, s32[2]{0:T(128)S(1)} %get-tuple-element.27.span_ref, ...), custom_call_target="tpu_custom_call" | custom-call | flops 4529848320 | bytes 37500000 | tf_op jit(solution)/shard_map/tile_sums/pallas_call | solution.py:90
  36.1 8.6 %collective-permute-done = f32[3,128,512]{2,1,0:T(8,128)S(1)} collective-permute-done((f32[3,128,512]{2,1,0:T(8,128)S(1)}, f32[3,128,512]{2,1,0:T(8,128)S(1)}, u32[]{:S(2)}, u32[]{:S(2)}) %collective-permute-start) | collective-permute-done | bytes 786464 | tf_op jit(solution)/shard_map/ppermute | solution.py:216
  44.7 0.1 add.134
  45.0 0.1 add.137
  45.1 2.7 collective-permute-start.4
  47.8 16.5 %collective-permute-done.1 = f32[3,128,512]{2,1,0:T(8,128)S(1)} collective-permute-done((f32[3,128,512]{2,1,0:T(8,128)S(1)}, f32[3,128,512]{2,1,0:T(8,128)S(1)}, u32[]{:S(2)}, u32[]{:S(2)}) %collective-permute-start.1) | collective-permute-done | bytes 786464 | tf_op jit(solution)/shard_map/ppermute | solution.py:216
  64.6 0.1 add.138
  64.7 2.9 collective-permute-start.5
  67.6 15.4 %collective-permute-done.2 = f32[3,128,512]{2,1,0:T(8,128)S(1)} collective-permute-done((f32[3,128,512]{2,1,0:T(8,128)S(1)}, f32[3,128,512]{2,1,0:T(8,128)S(1)}, u32[]{:S(2)}, u32[]{:S(2)}) %collective-permute-start.2) | collective-permute-done | bytes 786464 | tf_op jit(solution)/shard_map/ppermute | solution.py:216
  83.2 0.1 add.139
  83.3 3.7 convolution_bitcast_fusion
  87.0 1.3 pad_maximum_fusion
  88.3 261.8 %all-reduce.2.cloned.1.call-done.g_ref = f32[512,512]{1,0:T(8,128)} async-done(((f32[512,512]{1,0:T(8,128)}), f32[512,512]{1,0:T(8,128)}) %all-reduce.2.cloned.1.call-update) | async-done | bytes 1048592 | tf_op jit(solution)/shard_map/psum | solution.py:238
  350.1 26.3 %factor_solve.1 = (f32[768,512]{1,0:T(8,128)}, f32[512,512]{1,0:T(8,128)}) custom-call(f32[512,512]{1,0:T(8,128)} %all-reduce.2.cloned.1.call-done.g_ref, f32[768,512]{1,0:T(8,128)} %bitcast.14), custom_call_target="tpu_custom_call" | custom-call | tf_op jit(solution)/shard_map/factor_solve/pallas_call | solution.py:202
  (14 shorter events, 0.7 us)
Async XLA Ops:
  7.2 343.0 %all-reduce.2.cloned.1.call-start = ((), (), s32[]{:S(2)}) async-start(), calls=%async_computation | async-start | bytes 2097152 | tf_op jit(solution)/shard_map/psum | solution.py:238
  12.1 4.4 %copy-start = (bf16[1,1,360,128,128]{4,3,2,1,0:T(8,128)(2,1)S(1)}, bf16[1,1,360,128,128]{4,3,2,1,0:T(8,128)(2,1)}, u32[]{:S(2)}) copy-start(bf16[1,1,360,128,128]{4,3,2,1,0:T(8,128)(2,1)} %param.4) | copy-start | bytes 35389444
  21.3 23.4 %collective-permute-start = (f32[3,128,512]{2,1,0:T(8,128)S(1)}, f32[3,128,512]{2,1,0:T(8,128)S(1)}, u32[]{:S(2)}, u32[]{:S(2)}) collective-permute-start(f32[3,128,512]{2,1,0:T(8,128)S(1)} %get-tuple-element.10), channel_id=1, source_target_pairs={{0,1},{1,2},{2,3},{3,0},{4,5},{5,6},{6,7},{7,4},{8,9},{9,10},{10,1... | collective-permute-start | bytes 2359304 | tf_op jit(solution)/shard_map/ppermute | solution.py:216
  23.6 21.4 %collective-permute-start.3 = (f32[3,128,512]{2,1,0:T(8,128)S(1)}, f32[3,128,512]{2,1,0:T(8,128)S(1)}, u32[]{:S(2)}, u32[]{:S(2)}) collective-permute-start(f32[3,128,512]{2,1,0:T(8,128)S(1)} %get-tuple-element.14), channel_id=1, source_target_pairs={{0,3},{1,0},{2,1},{3,2},{4,7},{5,4},{6,5},{7,6},{8,11},{9,8},{10,9... | collective-permute-start | bytes 2359304 | tf_op jit(solution)/shard_map/ppermute | solution.py:216
  44.9 19.4 %collective-permute-start.1 = (f32[3,128,512]{2,1,0:T(8,128)S(1)}, f32[3,128,512]{2,1,0:T(8,128)S(1)}, u32[]{:S(2)}, u32[]{:S(2)}) collective-permute-start(f32[3,128,512]{2,1,0:T(8,128)S(1)} %add.134), channel_id=1, source_target_pairs={{0,1},{1,2},{2,3},{3,0},{4,5},{5,6},{6,7},{7,4},{8,9},{9,10},{10,1... | collective-permute-start | bytes 2359304 | tf_op jit(solution)/shard_map/ppermute | solution.py:216
  45.1 19.4 %collective-permute-start.4 = (f32[3,128,512]{2,1,0:T(8,128)S(1)}, f32[3,128,512]{2,1,0:T(8,128)S(1)}, u32[]{:S(2)}, u32[]{:S(2)}) collective-permute-start(f32[3,128,512]{2,1,0:T(8,128)S(1)} %add.137), channel_id=1, source_target_pairs={{0,3},{1,0},{2,1},{3,2},{4,7},{5,4},{6,5},{7,6},{8,11},{9,8},{10,9... | collective-permute-start | bytes 2359304 | tf_op jit(solution)/shard_map/ppermute | solution.py:216
  64.5 18.6 %collective-permute-start.2 = (f32[3,128,512]{2,1,0:T(8,128)S(1)}, f32[3,128,512]{2,1,0:T(8,128)S(1)}, u32[]{:S(2)}, u32[]{:S(2)}) collective-permute-start(f32[3,128,512]{2,1,0:T(8,128)S(1)} %add.135), channel_id=1, source_target_pairs={{0,1},{1,2},{2,3},{3,0},{4,5},{5,6},{6,7},{7,4},{8,9},{9,10},{10,1... | collective-permute-start | bytes 2359304 | tf_op jit(solution)/shard_map/ppermute | solution.py:216
  64.7 18.5 %collective-permute-start.5 = (f32[3,128,512]{2,1,0:T(8,128)S(1)}, f32[3,128,512]{2,1,0:T(8,128)S(1)}, u32[]{:S(2)}, u32[]{:S(2)}) collective-permute-start(f32[3,128,512]{2,1,0:T(8,128)S(1)} %add.138), channel_id=1, source_target_pairs={{0,3},{1,0},{2,1},{3,2},{4,7},{5,4},{6,5},{7,6},{8,11},{9,8},{10,9... | collective-permute-start | bytes 2359304 | tf_op jit(solution)/shard_map/ppermute | solution.py:216
Sparse Core Ops, SparseCore 0:
  87.2 262.9 all-reduce.1

commit v2 on v1

--- a/solution.py
+++ b/solution.py
@@ -97,7 +97,7 @@
                             pltpu.VMEM((nout * rows + 1, size, width), jnp.float32),
                             pltpu.SemaphoreType.DMA((RING, GROUP)), pltpu.SemaphoreType.DMA((RING, GROUP)), pltpu.SemaphoreType.DMA((nout,))]),
         out_shape=[jax.ShapeDtypeStruct((rows, size, width), jnp.float32)] * nout,
-        compiler_params=pltpu.CompilerParams(vmem_limit_bytes=40 << 20),
+        compiler_params=pltpu.CompilerParams(vmem_limit_bytes=60 << 20),
         cost_estimate=pl.CostEstimate(flops=2 * 360 * 128 * 128 * 512 * rows * nout // 24, bytes_accessed=50_000_000 * rows * nout // 24, transcendentals=0),
         name="tile_sums",
     )(plan, span, tiles, panels)
@@ -133,7 +133,119 @@
 def dot_hi(a, b, dims):
     return lax.dot_general(a, b, (dims, ((), ())), precision=HI, preferred_element_type=jnp.float32)
 
-def factor_block(a_ref, w_ref, u_ref, m):
+MESH = pl.DeviceIdType.MESH
+HALF = ((0, 1, 0, 1), (2, 1, 2, 1), (0, 1, 1, 1), (2, -2, 3, 0), (0, 1, 2, 1))
+
+def gram_kernel(dims, rows_ref, out_ref, part, mate, mine, inbox, tower, full, cs, cr, ps, pr, zs, zr, gs, gr, fs, fr):
+    zn, xn, yn = dims
+    row = lax.axis_index("row")
+    y = lax.axis_index("col")
+    core = lax.rem(row, 2)
+    x = lax.rem(row // 2, xn)
+    z = row // (2 * xn)
+    other = 1 - core
+
+    def at(zz, xx, yy, cc):
+        return ((zz * xn + xx) * 2 + cc, yy)
+
+    partner = at(z, x, y, other)
+    plane = []
+    for j in range(1, xn * yn):
+        dx, dy = j // yn, j % yn
+        plane.append((at(z, lax.rem(x + dx, xn), lax.rem(y + dy, yn), core),
+                      lax.rem(x + dx, xn) * yn + lax.rem(y + dy, yn),
+                      lax.rem(x + xn - dx, xn) * yn + lax.rem(y + yn - dy, yn)))
+    column = [at(lax.rem(z + j, zn), x, y, core) for j in range(1, zn)]
+    own = x * yn + y
+    piece = mine.shape[0] // (xn * yn)
+
+    barrier = pltpu.get_barrier_semaphore()
+    peers = [partner] + [p[0] for p in plane] + column
+    for peer in peers:
+        pl.semaphore_signal(barrier, inc=1, device_id=peer, device_id_type=MESH)
+
+    def fill(h):
+        for b, (i0, i1, j0, j1) in enumerate(HALF):
+            left = rows_ref[:, pl.ds(pl.multiple_of((i0 + i1 * h) * 128, 128), 128)]
+            right = rows_ref[:, pl.ds(pl.multiple_of((j0 + j1 * h) * 128, 128), 128)]
+            part[h, 128 * b:128 * b + 128, :] = dot_hi(left, right, ((0,), (0,)))
+
+    def remote(src, dst, send, recv, dev):
+        return pltpu.make_async_remote_copy(src_ref=src, dst_ref=dst, send_sem=send, recv_sem=recv, device_id=dev, device_id_type=MESH)
+
+    fill(other)
+    pl.semaphore_wait(barrier, len(peers))
+    swap = remote(part.at[other], mate, cs, cr, partner)
+    swap.start()
+    fill(core)
+    swap.wait_recv()
+    mine[...] = part[core] + mate[...]
+    order = sorted(range(len(plane)), key=lambda j: -(min((j + 1) // yn, xn - (j + 1) // yn) + min((j + 1) % yn, yn - (j + 1) % yn)))
+    scatter = []
+    for j in order:
+        dev, theirs, _ = plane[j]
+        c = remote(mine.at[pl.ds(pl.multiple_of(theirs * piece, 8), piece)], inbox.at[j], ps.at[j], pr.at[j], dev)
+        c.start()
+        scatter.append(c)
+    total = mine[pl.ds(pl.multiple_of(own * piece, 8), piece), :]
+    for j, c in zip(reversed(order), reversed(scatter)):
+        c.wait_recv()
+        total = total + inbox[j]
+    tower[z] = total
+    climb = []
+    for j in sorted(range(zn - 1), key=lambda j: -min(j + 1, zn - j - 1)):
+        c = remote(tower.at[z], tower.at[z], zs.at[j], zr.at[j], column[j])
+        c.start()
+        climb.append(c)
+    for c in climb:
+        c.wait_recv()
+    total = tower[0]
+    for k in range(1, zn):
+        total = total + tower[k]
+    full[core, own] = total
+    spread = {}
+    for j in order:
+        dev, _, _ = plane[j]
+        spread[j] = remote(full.at[core, own], full.at[core, own], gs.at[j], gr.at[j], dev)
+        spread[j].start()
+    hand = [remote(full.at[core, own], full.at[core, own], fs.at[len(plane)], fr.at[len(plane)], partner)]
+    hand[0].start()
+    for j in reversed(order):
+        spread[j].wait_recv()
+        source = plane[j][2]
+        c = remote(full.at[core, source], full.at[core, source], fs.at[j], fr.at[j], partner)
+        c.start()
+        hand.append(c)
+    for c in hand:
+        c.wait_recv()
+    out_ref[...] = full[...]
+    for c in [swap] + scatter + climb + list(spread.values()) + hand:
+        c.wait_send()
+
+def gram_sum(rows, dims):
+    zn, xn, yn = dims
+    n = rows.shape[1]
+    pieces = xn * yn
+    tall = 5 * 128
+    sem = pltpu.SemaphoreType.DMA
+    return pl.pallas_call(
+        functools.partial(gram_kernel, dims),
+        out_shape=jax.ShapeDtypeStruct((2, pieces, tall // pieces, 128), jnp.float32),
+        in_specs=[pl.BlockSpec(memory_space=pltpu.VMEM)],
+        out_specs=pl.BlockSpec(memory_space=pltpu.VMEM),
+        scratch_shapes=[pltpu.VMEM((2, tall, 128), jnp.float32), pltpu.VMEM((tall, 128), jnp.float32), pltpu.VMEM((tall, 128), jnp.float32),
+                        pltpu.VMEM((pieces - 1, tall // pieces, 128), jnp.float32), pltpu.VMEM((zn, tall // pieces, 128), jnp.float32),
+                        pltpu.VMEM((2, pieces, tall // pieces, 128), jnp.float32),
+                        sem, sem, sem((pieces - 1,)), sem((pieces - 1,)), sem((zn - 1,)), sem((zn - 1,)),
+                        sem((pieces - 1,)), sem((pieces - 1,)), sem((pieces,)), sem((pieces,))],
+        compiler_params=pltpu.CompilerParams(collective_id=0, has_side_effects=True),
+        name="gram_sum",
+    )(rows)
+
+BLOCKS = tuple(tuple((i0 + i1 * h, j0 + j1 * h) for i0, i1, j0, j1 in HALF) for h in range(2))
+
+
+def factor_block(a_ref, w_ref, u_ref):
     n = 128
     nv = n // 8
     lane = lax.broadcasted_iota(jnp.int32, (8, n), 1)
@@ -177,25 +289,30 @@
         w_ref[8 * r:8 * r + 8, :] = ub
 
 def chol_kernel(scale, g_ref, s_ref, x_ref, t_ref, gw, xs, d_ref, w_ref, u_ref):
-    n = g_ref.shape[0]
+    n = gw.shape[0]
     nb = n // 128
-    gw[...] = g_ref[...]
+    for h in range(2):
+        for b, (i, j) in enumerate(BLOCKS[h]):
+            gw[128 * i:128 * i + 128, 128 * j:128 * j + 128] = g_ref[h, b]
     xs[...] = s_ref[...] * scale
     t_ref[...] = jnp.zeros_like(t_ref)
     for k in range(nb):
         lo = 128 * k
         hi = lo + 128
         d_ref[...] = gw[lo:hi, lo:hi]
-        factor_block(d_ref, w_ref, u_ref, k)
+        factor_block(d_ref, w_ref, u_ref)
         w = w_ref[...]
         t_ref[lo:hi, lo:hi] = u_ref[...] * (1.0 / scale)
+        if hi < n:
+            up = dot_hi(w, gw[lo:hi, hi:n], ((1,), (0,)))
+            t_ref[lo:hi, hi:n] = up * (1.0 / scale)
+            for i in range(hi, n, 128):
+                gw[i:i + 128, i:n] = gw[i:i + 128, i:n] - dot_hi(up[:, i - hi:i - hi + 128], up[:, i - hi:], ((0,), (0,)))
         xk = dot_hi(xs[:, lo:hi], w, ((1,), (1,)))
         x_ref[:, lo:hi] = xk
         if hi < n:
-            up = dot_hi(w, gw[lo:hi, hi:n], ((1,), (0,)))
-            t_ref[lo:hi, hi:n] = up * (1.0 / scale)
-            gw[hi:n, hi:n] = gw[hi:n, hi:n] - dot_hi(up, up, ((0,), (0,)))
             xs[:, hi:n] = xs[:, hi:n] - dot_hi(xk, up, ((1,), (0,)))
+
 
 def chol_solve(gram, rows, scale):
     m, n = rows.shape
@@ -234,10 +351,9 @@
         up = shifted(up, 1) + later[2 * turn]
         down = shifted(down, -1) + later[2 * turn + 1]
     own_rows = jnp.concatenate([up, down], axis=0).reshape(local_rows, sketch_width)
-    gram_local = jnp.dot(own_rows.T, own_rows, precision=HI, preferred_element_type=jnp.float32)
-    gram_whole = lax.psum(gram_local, ("row", "col"))
+    gram_blocks = gram_sum(own_rows, (row_devices // 8, 4, col_devices)).reshape(2, 5, 128, 128)
     order_scale = math.sqrt(local_rows * row_devices * col_devices)
-    basis_rows, upper = chol_solve(gram_whole, own_rows, order_scale)
+    basis_rows, upper = chol_solve(gram_blocks, own_rows, order_scale)
     return basis_rows, upper
 
 

time: 383 us -> 139 us (0.36)
  waiting for transfers between devices: 302 us -> 32.1 us
  Pallas kernels: 40 us -> 80 us
  between operations: 14.8 us -> 1.43 us
  starting transfers between devices: 11.8 us -> 16.2 us
  local copies, waits for them, and re-layouts: 4.35 us -> 0.02 us
    psum x1 -> x0, waiting for transfers between devices: 262 us -> none  [body(): gram_whole = lax.psum(gram_local, ('row', 'col'))]
    pallas_call x0 -> x1, Pallas kernels: none -> 38.8 us  [gram_sum(): pl.pallas_call(functools.partial(gram_kernel, dims), out_shape=jax.ShapeD...]
    ppermute x6, waiting for transfers between devices: 40.5 us -> 32.1 us  [shifted(): lax.ppermute(block, 'col', [(i, (i + distance) % count) for i in range(co...]
    ppermute x6, starting transfers between devices: 11.8 us -> 16.2 us  [shifted(): lax.ppermute(block, 'col', [(i, (i + distance) % count) for i in range(co...]
    unnamed x2 -> x10, local copies, waits for them, and re-layouts: 4.35 us -> 0.02 us
  transfers between devices with their start and end apart: 7 -> 6, of which waited for: 4 -> 3; matrix products, arithmetic and copies ran while one was open for 1% -> 1% of each run, Pallas kernels for 2% -> 7%
where the time goes in v2:
time: 139 us; the launch traced here: 138 us
  Pallas kernels  80 us (58%)
  waiting for transfers between devices  32.1 us (23%)
  starting transfers between devices  16.2 us (12%)
  other arithmetic  8.71 us (6%)
  between operations  1.43 us (1%)
    pallas_call x1, Pallas kernels, gram_sum(): pl.pallas_call(functools.partial(gram_kernel, dims), out_shape=jax.ShapeD...  38.8 us
    ppermute x6, waiting for transfers between devices, shifted(): lax.ppermute(block, 'col', [(i, (i + distance) % count) for i in range(co...  32.1 us
    pallas_call x1, Pallas kernels, chol_solve(): pl.pallas_call(functools.partial(chol_kernel, scale), out_shape=(jax.Shap...  25 us
    ppermute x6, starting transfers between devices, shifted(): lax.ppermute(block, 'col', [(i, (i + distance) % count) for i in range(co...  16.2 us
    pallas_call x2, Pallas kernels, sparse_sum(): pl.pallas_call(functools.partial(sparse_kernel, base), grid_spec=pltpu.Pr...  16.1 us
  transfers between devices with their start and end apart: 6, of which 3 were waited for; matrix products, arithmetic and copies ran while one was open for 1% of the time, Pallas kernels for 7%

profile of v2, /device:TPU:1, one launch (start us, length us, event | category | flops | bytes accessed | tf_op | source)
XLA Modules:
  0.0 138.4 jit_solution(10716842337355472558)
XLA Ops:
  0.6 0.7 compare_reduce_fusion
  1.3 0.8 shift-left_reduce_fusion
  2.9 0.2 convert_reduce_fusion
  3.1 0.7 fusion.8
  4.0 0.7 select_reduce_fusion.plan_ref
  4.7 2.0 %pad_add_fusion = (s32[2]{0:T(128)}, s32[2]{0:T(128)}) fusion(s32[1]{0:T(128)} %bitcast.1, s32[1]{0:T(128)} %constant.79.clone.1, s32[1]{0:T(128)} %bitcast.4), kind=kLoop, calls=%fused_computation.37 | loop fusion | flops 4 | bytes 28 | tf_op jit(solution)/shard_map/stack | solution.py:128
  6.7 6.1 %tile_sums.2 = (f32[3,128,512]{2,1,0:T(8,128)}, f32[3,128,512]{2,1,0:T(8,128)}) custom-call(s32[512]{0:T(512)} %select_reduce_fusion.plan_ref, s32[2]{0:T(128)} %get-tuple-element.26.span_ref, bf16[360,128,128]{2,1,0:T(8,128)(2,1)} %bitcast.11, bf16[384,128,512]{2,1,0:T(8,128)(2,1)} %bitcast.9), custom_call_target="tpu_custom_call" | custom-call | flops 1509949440 | bytes 12500000 | tf_op jit(solution)/shard_map/tile_sums/pallas_call | solution.py:90
  12.8 2.3 %collective-permute-start = (f32[3,128,512]{2,1,0:T(8,128)}, f32[3,128,512]{2,1,0:T(8,128)S(1)}, u32[]{:S(2)}, u32[]{:S(2)}) collective-permute-start(f32[3,128,512]{2,1,0:T(8,128)} %get-tuple-element.10), channel_id=1, source_target_pairs={{0,1},{1,2},{2,3},{3,0},{4,5},{5,6},{6,7},{7,4},{8,9},{9,10},{10,1... | collective-permute-start | bytes 2359304 | tf_op jit(solution)/shard_map/ppermute | solution.py:333
  15.1 3.4 %collective-permute-start.3 = (f32[3,128,512]{2,1,0:T(8,128)}, f32[3,128,512]{2,1,0:T(8,128)S(1)}, u32[]{:S(2)}, u32[]{:S(2)}) collective-permute-start(f32[3,128,512]{2,1,0:T(8,128)} %get-tuple-element.14), channel_id=1, source_target_pairs={{0,3},{1,0},{2,1},{3,2},{4,7},{5,4},{6,5},{7,6},{8,11},{9,8},{10,9... | collective-permute-start | bytes 2359304 | tf_op jit(solution)/shard_map/ppermute | solution.py:333
  18.6 10.0 %tile_sums.3 = (f32[3,128,512]{2,1,0:T(8,128)}, f32[3,128,512]{2,1,0:T(8,128)}, f32[3,128,512]{2,1,0:T(8,128)}, f32[3,128,512]{2,1,0:T(8,128)}, f32[3,128,512]{2,1,0:T(8,128)}, /*index=5*/f32[3,128,512]{2,1,0:T(8,128)}) custom-call(s32[512]{0:T(512)} %select_reduce_fusion.plan_ref, s32[2]{0:T(128)} %get-tuple-element.27.span_ref, ...), custom_call_target="tpu_custom_call" | custom-call | flops 4529848320 | bytes 37500000 | tf_op jit(solution)/shard_map/tile_sums/pallas_call | solution.py:90
  28.6 4.9 %collective-permute-done = f32[3,128,512]{2,1,0:T(8,128)S(1)} collective-permute-done((f32[3,128,512]{2,1,0:T(8,128)}, f32[3,128,512]{2,1,0:T(8,128)S(1)}, u32[]{:S(2)}, u32[]{:S(2)}) %collective-permute-start) | collective-permute-done | bytes 786464 | tf_op jit(solution)/shard_map/ppermute | solution.py:333
  33.6 1.3 add.132
  35.0 0.1 add.135
  35.1 4.0 %collective-permute-start.4 = (f32[3,128,512]{2,1,0:T(8,128)S(1)}, f32[3,128,512]{2,1,0:T(8,128)S(1)}, u32[]{:S(2)}, u32[]{:S(2)}) collective-permute-start(f32[3,128,512]{2,1,0:T(8,128)S(1)} %add.135), channel_id=1, source_target_pairs={{0,3},{1,0},{2,1},{3,2},{4,7},{5,4},{6,5},{7,6},{8,11},{9,8},{10,9... | collective-permute-start | bytes 2359304 | tf_op jit(solution)/shard_map/ppermute | solution.py:333
  39.2 12.5 %collective-permute-done.1 = f32[3,128,512]{2,1,0:T(8,128)S(1)} collective-permute-done((f32[3,128,512]{2,1,0:T(8,128)S(1)}, f32[3,128,512]{2,1,0:T(8,128)S(1)}, u32[]{:S(2)}, u32[]{:S(2)}) %collective-permute-start.1) | collective-permute-done | bytes 786464 | tf_op jit(solution)/shard_map/ppermute | solution.py:333
  51.8 0.2 collective-permute-start.2
  52.0 0.1 add.136
  52.2 6.1 %collective-permute-start.5 = (f32[3,128,512]{2,1,0:T(8,128)S(1)}, f32[3,128,512]{2,1,0:T(8,128)S(1)}, u32[]{:S(2)}, u32[]{:S(2)}) collective-permute-start(f32[3,128,512]{2,1,0:T(8,128)S(1)} %add.136), channel_id=1, source_target_pairs={{0,3},{1,0},{2,1},{3,2},{4,7},{5,4},{6,5},{7,6},{8,11},{9,8},{10,9... | collective-permute-start | bytes 2359304 | tf_op jit(solution)/shard_map/ppermute | solution.py:333
  58.3 14.7 %collective-permute-done.2 = f32[3,128,512]{2,1,0:T(8,128)S(1)} collective-permute-done((f32[3,128,512]{2,1,0:T(8,128)S(1)}, f32[3,128,512]{2,1,0:T(8,128)S(1)}, u32[]{:S(2)}, u32[]{:S(2)}) %collective-permute-start.2) | collective-permute-done | bytes 786464 | tf_op jit(solution)/shard_map/ppermute | solution.py:333
  73.0 0.1 add.134
  73.1 0.1 add.137
  73.3 1.3 pad_maximum_fusion
  74.6 38.8 %gram_sum.1 = f32[2,16,40,128]{3,2,1,0:T(8,128)} custom-call(f32[768,512]{1,0:T(8,128)} %bitcast.13), custom_call_target="tpu_custom_call" | custom-call | tf_op jit(solution)/shard_map/gram_sum/pallas_call | solution.py:231
  113.4 25.0 %factor_solve.1 = (f32[768,512]{1,0:T(8,128)}, f32[512,512]{1,0:T(8,128)}) custom-call(f32[2,5,128,128]{3,2,1,0:T(8,128)} %bitcast.15, f32[768,512]{1,0:T(8,128)} %bitcast.14), custom_call_target="tpu_custom_call" | custom-call | tf_op jit(solution)/shard_map/factor_solve/pallas_call | solution.py:319
  (19 shorter events, 0.5 us)
Async XLA Ops:
  12.8 20.7 %collective-permute-start = (f32[3,128,512]{2,1,0:T(8,128)}, f32[3,128,512]{2,1,0:T(8,128)S(1)}, u32[]{:S(2)}, u32[]{:S(2)}) collective-permute-start(f32[3,128,512]{2,1,0:T(8,128)} %get-tuple-element.10), channel_id=1, source_target_pairs={{0,1},{1,2},{2,3},{3,0},{4,5},{5,6},{6,7},{7,4},{8,9},{9,10},{10,1... | collective-permute-start | bytes 2359304 | tf_op jit(solution)/shard_map/ppermute | solution.py:333
  15.1 19.8 %collective-permute-start.3 = (f32[3,128,512]{2,1,0:T(8,128)}, f32[3,128,512]{2,1,0:T(8,128)S(1)}, u32[]{:S(2)}, u32[]{:S(2)}) collective-permute-start(f32[3,128,512]{2,1,0:T(8,128)} %get-tuple-element.14), channel_id=1, source_target_pairs={{0,3},{1,0},{2,1},{3,2},{4,7},{5,4},{6,5},{7,6},{8,11},{9,8},{10,9... | collective-permute-start | bytes 2359304 | tf_op jit(solution)/shard_map/ppermute | solution.py:333
  28.6 6.3 %copy-start.4 = (f32[3,128,512]{2,1,0:T(8,128)S(1)}, f32[3,128,512]{2,1,0:T(8,128)}, u32[]{:S(2)}) copy-start(f32[3,128,512]{2,1,0:T(8,128)} %get-tuple-element.15) | copy-start | bytes 2359300
  34.8 16.8 %copy-start.3 = (f32[3,128,512]{2,1,0:T(8,128)S(1)}, f32[3,128,512]{2,1,0:T(8,128)}, u32[]{:S(2)}) copy-start(f32[3,128,512]{2,1,0:T(8,128)} %get-tuple-element.12) | copy-start | bytes 2359300
  34.8 16.8 %collective-permute-start.1 = (f32[3,128,512]{2,1,0:T(8,128)S(1)}, f32[3,128,512]{2,1,0:T(8,128)S(1)}, u32[]{:S(2)}, u32[]{:S(2)}) collective-permute-start(f32[3,128,512]{2,1,0:T(8,128)S(1)} %add.132), channel_id=1, source_target_pairs={{0,1},{1,2},{2,3},{3,0},{4,5},{5,6},{6,7},{7,4},{8,9},{9,10},{10,1... | collective-permute-start | bytes 2359304 | tf_op jit(solution)/shard_map/ppermute | solution.py:333
  35.1 16.9 %copy-start.2 = (f32[3,128,512]{2,1,0:T(8,128)S(1)}, f32[3,128,512]{2,1,0:T(8,128)}, u32[]{:S(2)}) copy-start(f32[3,128,512]{2,1,0:T(8,128)} %get-tuple-element.16) | copy-start | bytes 2359300
  35.1 16.9 %collective-permute-start.4 = (f32[3,128,512]{2,1,0:T(8,128)S(1)}, f32[3,128,512]{2,1,0:T(8,128)S(1)}, u32[]{:S(2)}, u32[]{:S(2)}) collective-permute-start(f32[3,128,512]{2,1,0:T(8,128)S(1)} %add.135), channel_id=1, source_target_pairs={{0,3},{1,0},{2,1},{3,2},{4,7},{5,4},{6,5},{7,6},{8,11},{9,8},{10,9... | collective-permute-start | bytes 2359304 | tf_op jit(solution)/shard_map/ppermute | solution.py:333
  51.8 21.2 %copy-start.1 = (f32[3,128,512]{2,1,0:T(8,128)S(1)}, f32[3,128,512]{2,1,0:T(8,128)}, u32[]{:S(2)}) copy-start(f32[3,128,512]{2,1,0:T(8,128)} %get-tuple-element.13) | copy-start | bytes 2359300
  51.8 21.2 %collective-permute-start.2 = (f32[3,128,512]{2,1,0:T(8,128)S(1)}, f32[3,128,512]{2,1,0:T(8,128)S(1)}, u32[]{:S(2)}, u32[]{:S(2)}) collective-permute-start(f32[3,128,512]{2,1,0:T(8,128)S(1)} %add.133), channel_id=1, source_target_pairs={{0,1},{1,2},{2,3},{3,0},{4,5},{5,6},{6,7},{7,4},{8,9},{9,10},{10,1... | collective-permute-start | bytes 2359304 | tf_op jit(solution)/shard_map/ppermute | solution.py:333
  52.2 21.0 %copy-start = (f32[3,128,512]{2,1,0:T(8,128)S(1)}, f32[3,128,512]{2,1,0:T(8,128)}, u32[]{:S(2)}) copy-start(f32[3,128,512]{2,1,0:T(8,128)} %get-tuple-element.17) | copy-start | bytes 2359300
  52.2 21.0 %collective-permute-start.5 = (f32[3,128,512]{2,1,0:T(8,128)S(1)}, f32[3,128,512]{2,1,0:T(8,128)S(1)}, u32[]{:S(2)}, u32[]{:S(2)}) collective-permute-start(f32[3,128,512]{2,1,0:T(8,128)S(1)} %add.136), channel_id=1, source_target_pairs={{0,3},{1,0},{2,1},{3,2},{4,7},{5,4},{6,5},{7,6},{8,11},{9,8},{10,9... | collective-permute-start | bytes 2359304 | tf_op jit(solution)/shard_map/ppermute | solution.py:333

commit v3 on v2

--- a/solution.py
+++ b/solution.py
@@ -134,9 +134,12 @@
     return lax.dot_general(a, b, (dims, ((), ())), precision=HI, preferred_element_type=jnp.float32)
 
 MESH = pl.DeviceIdType.MESH
-HALF = ((0, 1, 0, 1), (2, 1, 2, 1), (0, 1, 1, 1), (2, -2, 3, 0), (0, 1, 2, 1))
-
-def gram_kernel(dims, rows_ref, out_ref, part, mate, mine, inbox, tower, full, cs, cr, ps, pr, zs, zr, gs, gr, fs, fr):
+BLOCKS = (((0, 0), (2, 2), (0, 1), (2, 3), (0, 2)), ((1, 1), (3, 3), (1, 2), (0, 3), (1, 3)))
+SPOT = {ij: (h, b) for h in range(2) for b, ij in enumerate(BLOCKS[h])}
+
+def ring_kernel(dims, up_ref, down_ref, later_ref, rows_ref, out_ref,
+                head, later, box1, box2, part, mate, mine, inbox, tower, full,
+                hsem, lsem, s1, r1, s2, r2, cs, cr, ps, pr, zs, zr, gs, gr, fs, fr):
     zn, xn, yn = dims
     row = lax.axis_index("row")
     y = lax.axis_index("col")
@@ -144,6 +147,8 @@
     x = lax.rem(row // 2, xn)
     z = row // (2 * xn)
     other = 1 - core
+    count = up_ref.shape[0]
+    tall = up_ref.shape[1]
 
     def at(zz, xx, yy, cc):
         return ((zz * xn + xx) * 2 + cc, yy)
@@ -158,26 +163,77 @@
     column = [at(lax.rem(z + j, zn), x, y, core) for j in range(1, zn)]
     own = x * yn + y
     piece = mine.shape[0] // (xn * yn)
+    ring = [(row, lax.rem(y + 1, yn)), (row, lax.rem(y + yn - 1, yn))]
 
     barrier = pltpu.get_barrier_semaphore()
     peers = [partner] + [p[0] for p in plane] + column
     for peer in peers:
         pl.semaphore_signal(barrier, inc=1, device_id=peer, device_id_type=MESH)
 
-    def fill(h):
-        for b, (i0, i1, j0, j1) in enumerate(HALF):
-            left = rows_ref[:, pl.ds(pl.multiple_of((i0 + i1 * h) * 128, 128), 128)]
-            right = rows_ref[:, pl.ds(pl.multiple_of((j0 + j1 * h) * 128, 128), 128)]
-            part[h, 128 * b:128 * b + 128, :] = dot_hi(left, right, ((0,), (0,)))
-
     def remote(src, dst, send, recv, dev):
         return pltpu.make_async_remote_copy(src_ref=src, dst_ref=dst, send_sem=send, recv_sem=recv, device_id=dev, device_id_type=MESH)
 
-    fill(other)
+    def head_copy(i, d):
+        return pltpu.make_async_copy((up_ref, down_ref)[d].at[i], head.at[d, i], hsem.at[d, i])
+
+    def later_copy(step, i, d):
+        p = (2 * step + d) * count + i
+        return pltpu.make_async_copy(later_ref.at[p], later.at[step, d, i], lsem.at[step, d, i])
+
+    def hop1(i, d):
+        return remote(head.at[d, i], box1.at[d, i], s1.at[d, i], r1.at[d, i], ring[d])
+
+    def hop2(i, d):
+        return remote(box1.at[d, i], box2.at[d, i], s2.at[d, i], r2.at[d, i], ring[d])
+
+    for i in range(count):
+        for d in range(2):
+            head_copy(i, d).start()
+            later_copy(0, i, d).start()
+    for step in range(1, 3):
+        for i in range(count):
+            for d in range(2):
+                later_copy(step, i, d).start()
+    part[...] = jnp.zeros_like(part)
     pl.semaphore_wait(barrier, len(peers))
+
+    def first(i, c):
+        for d in range(2):
+            head_copy(i, d).wait()
+            later_copy(0, i, d).wait()
+            head[d, i] = head[d, i] + later[0, d, i]
+            hop1(i, d).start()
+        return c
+
+    lax.fori_loop(0, count, first, 0)
+
+    def second(i, c):
+        for d in range(2):
+            later_copy(1, i, d).wait()
+            hop1(i, d).wait_recv()
+            box1[d, i] = box1[d, i] + later[1, d, i]
+            hop2(i, d).start()
+        return c
+
+    lax.fori_loop(0, count, second, 0)
+
+    def third(i, c):
+        for d in range(2):
+            later_copy(2, i, d).wait()
+            hop2(i, d).wait_recv()
+            total = box2[d, i] + later[2, d, i]
+            rows_ref[d, i] = total
+            for a in range(4):
+                got = dot_hi(total[:, 128 * a:128 * a + 128], total[:, 128 * a:], ((0,), (0,)))
+                for j in range(a, 4):
+                    h, b = SPOT[a, j]
+                    part[h, 128 * b:128 * b + 128, :] = part[h, 128 * b:128 * b + 128, :] + got[:, 128 * (j - a):128 * (j - a) + 128]
+        return c
+
+    lax.fori_loop(0, count, third, 0)
+
     swap = remote(part.at[other], mate, cs, cr, partner)
     swap.start()
-    fill(core)
     swap.wait_recv()
     mine[...] = part[core] + mate[...]
     order = sorted(range(len(plane)), key=lambda j: -(min((j + 1) // yn, xn - (j + 1) // yn) + min((j + 1) % yn, yn - (j + 1) % yn)))
@@ -222,27 +278,37 @@
     for c in [swap] + scatter + climb + list(spread.values()) + hand:
         c.wait_send()
 
-def gram_sum(rows, dims):
+    def drain(i, c):
+        for d in range(2):
+            hop1(i, d).wait_send()
+            hop2(i, d).wait_send()
+        return c
+
+    lax.fori_loop(0, count, drain, 0)
+
+def ring_sum(up, down, later, dims):
     zn, xn, yn = dims
-    n = rows.shape[1]
+    count, tall, n = up.shape
     pieces = xn * yn
-    tall = 5 * 128
+    deep = 5 * 128
     sem = pltpu.SemaphoreType.DMA
+    f32 = jnp.float32
     return pl.pallas_call(
-        functools.partial(gram_kernel, dims),
-        out_shape=jax.ShapeDtypeStruct((2, pieces, tall // pieces, 128), jnp.float32),
-        in_specs=[pl.BlockSpec(memory_space=pltpu.VMEM)],
-        out_specs=pl.BlockSpec(memory_space=pltpu.VMEM),
-        scratch_shapes=[pltpu.VMEM((2, tall, 128), jnp.float32), pltpu.VMEM((tall, 128), jnp.float32), pltpu.VMEM((tall, 128), jnp.float32),
-                        pltpu.VMEM((pieces - 1, tall // pieces, 128), jnp.float32), pltpu.VMEM((zn, tall // pieces, 128), jnp.float32),
-                        pltpu.VMEM((2, pieces, tall // pieces, 128), jnp.float32),
+        functools.partial(ring_kernel, dims),
+        out_shape=(jax.ShapeDtypeStruct((2, count, tall, n), f32), jax.ShapeDtypeStruct((2, pieces, deep // pieces, 128), f32)),
+        in_specs=[pl.BlockSpec(memory_space=pl.ANY)] * 3,
+        out_specs=(pl.BlockSpec(memory_space=pltpu.VMEM),) * 2,
+        scratch_shapes=[pltpu.VMEM((2, count, tall, n), f32), pltpu.VMEM((3, 2, count, tall, n), f32),
+                        pltpu.VMEM((2, count, tall, n), f32), pltpu.VMEM((2, count, tall, n), f32),
+                        pltpu.VMEM((2, deep, 128), f32), pltpu.VMEM((deep, 128), f32), pltpu.VMEM((deep, 128), f32),
+                        pltpu.VMEM((pieces - 1, deep // pieces, 128), f32), pltpu.VMEM((zn, deep // pieces, 128), f32),
+                        pltpu.VMEM((2, pieces, deep // pieces, 128), f32),
+                        sem((2, count)), sem((3, 2, count)), sem((2, count)), sem((2, count)), sem((2, count)), sem((2, count)),
                         sem, sem, sem((pieces - 1,)), sem((pieces - 1,)), sem((zn - 1,)), sem((zn - 1,)),
                         sem((pieces - 1,)), sem((pieces - 1,)), sem((pieces,)), sem((pieces,))],
-        compiler_params=pltpu.CompilerParams(collective_id=0, has_side_effects=True),
-        name="gram_sum",
-    )(rows)
-
-BLOCKS = tuple(tuple((i0 + i1 * h, j0 + j1 * h) for i0, i1, j0, j1 in HALF) for h in range(2))
+        compiler_params=pltpu.CompilerParams(collective_id=0, has_side_effects=True, vmem_limit_bytes=60 << 20),
+        name="ring_sum",
+    )(up, down, later)
 
 
 def factor_block(a_ref, w_ref, u_ref):
@@ -346,12 +412,10 @@
     me = lax.axis_index("col")
     plan, span0, span1 = make_plan(tile_places[0, 0], tile_counts[0, 0], me, col_devices, chunk_rows)
     up, down = sparse_sum(plan, span0, tile_stack, panels, 0, (2, half))
-    later = sparse_sum(plan, span1, tile_stack, panels, chunk_rows, (2 * (col_devices - 1), half))
-    for turn in range(col_devices - 1):
-        up = shifted(up, 1) + later[2 * turn]
-        down = shifted(down, -1) + later[2 * turn + 1]
-    own_rows = jnp.concatenate([up, down], axis=0).reshape(local_rows, sketch_width)
-    gram_blocks = gram_sum(own_rows, (row_devices // 8, 4, col_devices)).reshape(2, 5, 128, 128)
+    (later,) = sparse_sum(plan, span1, tile_stack, panels, chunk_rows, (1, chunk_rows * (col_devices - 1)))
+    own, gram = ring_sum(shifted(up, 1), shifted(down, -1), later, (row_devices // 8, 4, col_devices))
+    own_rows = own.reshape(local_rows, sketch_width)
+    gram_blocks = gram.reshape(2, 5, 128, 128)
     order_scale = math.sqrt(local_rows * row_devices * col_devices)
     basis_rows, upper = chol_solve(gram_blocks, own_rows, order_scale)
     return basis_rows, upper

time: 139 us -> 135 us (0.971)
  Pallas kernels: 80 us -> 122 us
  waiting for transfers between devices: 32.1 us -> 1.2 us
  starting transfers between devices: 16.2 us -> 2.75 us
  other arithmetic: 8.71 us -> 6.48 us
    pallas_call x1, Pallas kernels: 38.8 us -> 78.7 us  [ring_sum(): pl.pallas_call(functools.partial(ring_kernel, dims), out_shape=(jax.Shape...]
    ppermute x6 -> x2, waiting for transfers between devices: 32.1 us -> 1.2 us  [shifted(): lax.ppermute(block, 'col', [(i, (i + distance) % count) for i in range(co...]
    ppermute x6 -> x2, starting transfers between devices: 16.2 us -> 2.75 us  [shifted(): lax.ppermute(block, 'col', [(i, (i + distance) % count) for i in range(co...]
    pallas_call x2, Pallas kernels: 16.1 us -> 18.5 us  [sparse_sum(): pl.pallas_call(functools.partial(sparse_kernel, base), grid_spec=pltpu.Pr...]
    add x6 -> x0, other arithmetic: 1.98 us -> none  [the longest x3 1.56 us: body(): up = shifted(up, 1) + later[2 * turn]]
    another operation x1 -> x2, other arithmetic: 1.99 us -> 3.06 us  [make_plan(): return (plan, jnp.stack([jnp.int32(0), n0]), jnp.stack([n0, n1]))]
  transfers between devices with their start and end apart: 6 -> 2, of which waited for: 3 -> 1; matrix products, arithmetic and copies ran while one was open for 1% -> 1% of each run, Pallas kernels for 7% -> 9%
where the time goes in v3:
time: 135 us
  Pallas kernels  122 us (90%)
  other arithmetic  6.48 us (5%)
  starting transfers between devices  2.75 us (2%)
    pallas_call x1, Pallas kernels, ring_sum(): pl.pallas_call(functools.partial(ring_kernel, dims), out_shape=(jax.Shape...  78.7 us
    pallas_call x1, Pallas kernels, chol_solve(): pl.pallas_call(functools.partial(chol_kernel, scale), out_shape=(jax.Shap...  25 us
    pallas_call x2, Pallas kernels, sparse_sum(): pl.pallas_call(functools.partial(sparse_kernel, base), grid_spec=pltpu.Pr...  18.5 us
    another operation x2, other arithmetic, make_plan(): return (plan, jnp.stack([jnp.int32(0), n0]), jnp.stack([n0, n1]))  3.06 us
    ppermute x2, starting transfers between devices, shifted(): lax.ppermute(block, 'col', [(i, (i + distance) % count) for i in range(co...  2.75 us
  transfers between devices with their start and end apart: 2, of which 1 were waited for; matrix products, arithmetic and copies ran while one was open for 1% of the time, Pallas kernels for 9%

profile of v3, /device:TPU:1, one launch (start us, length us, event | category | flops | bytes accessed | tf_op | source)
XLA Modules:
  0.0 134.9 jit_solution(16748838961178206011)
XLA Ops:
  0.6 0.7 compare_reduce_fusion
  1.3 0.8 shift-left_reduce_fusion
  2.8 0.1 convert_reduce_fusion.1
  2.9 0.2 convert_reduce_fusion
  3.1 0.7 fusion.8
  3.9 0.1 select_reduce_fusion.1
  4.0 1.2 pad_add_fusion.span_ref
  5.1 0.7 select_reduce_fusion.plan_ref
  5.9 6.2 %tile_sums.2 = (f32[3,128,512]{2,1,0:T(8,128)}, f32[3,128,512]{2,1,0:T(8,128)}) custom-call(s32[512]{0:T(512)} %select_reduce_fusion.plan_ref, s32[2]{0:T(128)} %pad_add_fusion.span_ref, bf16[360,128,128]{2,1,0:T(8,128)(2,1)} %bitcast.11, bf16[384,128,512]{2,1,0:T(8,128)(2,1)} %bitcast.9), custom_call_target="tpu_custom_call" | custom-call | flops 1509949440 | bytes 12500000 | tf_op jit(solution)/shard_map/tile_sums/pallas_call | solution.py:90
  12.1 1.7 %collective-permute-start = (f32[3,128,512]{2,1,0:T(8,128)}, f32[3,128,512]{2,1,0:T(8,128)S(1)}, u32[]{:S(2)}, u32[]{:S(2)}) collective-permute-start(f32[3,128,512]{2,1,0:T(8,128)} %get-tuple-element.6), channel_id=1, source_target_pairs={{0,1},{1,2},{2,3},{3,0},{4,5},{5,6},{6,7},{7,4},{8,9},{9,10},{10,1... | collective-permute-start | bytes 2359304 | tf_op jit(solution)/shard_map/ppermute | solution.py:399
  13.8 1.0 collective-permute-start.1
  14.8 1.9 %pad_add_fusion.1.span_ref = s32[2]{0:T(128)} fusion(s32[1]{0:T(128)} %bitcast.4, s32[1]{0:T(128)} %bitcast.1), kind=kLoop, calls=%fused_computation.37 | loop fusion | flops 2 | bytes 16 | tf_op jit(solution)/shard_map/stack | solution.py:128
  16.7 12.4 %tile_sums.3.later_ref = f32[18,128,512]{2,1,0:T(8,128)} custom-call(s32[512]{0:T(512)} %select_reduce_fusion.plan_ref, s32[2]{0:T(128)} %pad_add_fusion.1.span_ref, bf16[360,128,128]{2,1,0:T(8,128)(2,1)} %bitcast.12, bf16[384,128,512]{2,1,0:T(8,128)(2,1)} %bitcast.10), custom_call_target="tpu_custom_call" | custom-call | flops 4529848320 | bytes 37500000 | tf_op jit(solution)/shard_map/tile_sums/pallas_call | solution.py:90
  29.1 0.0 collective-permute-done.up_ref
  29.1 0.0 copy-start
  29.1 1.2 collective-permute-done.1.down_ref
  30.3 0.0 copy-done
  30.3 0.0 copy-start.1
  30.3 0.9 copy-done.1
  31.2 78.7 %ring_sum.1 = (f32[2,3,128,512]{3,2,1,0:T(8,128)}, f32[2,16,40,128]{3,2,1,0:T(8,128)}) custom-call(f32[3,128,512]{2,1,0:T(8,128)} %copy-done, f32[3,128,512]{2,1,0:T(8,128)} %copy-done.1, f32[18,128,512]{2,1,0:T(8,128)} %tile_sums.3.later_ref), custom_call_target="tpu_custom_call" | custom-call | tf_op jit(solution)/shard_map/ring_sum/pallas_call | solution.py:296
  109.9 25.0 %factor_solve.1 = (f32[768,512]{1,0:T(8,128)}, f32[512,512]{1,0:T(8,128)}) custom-call(f32[2,5,128,128]{3,2,1,0:T(8,128)} %bitcast.14, f32[768,512]{1,0:T(8,128)} %bitcast.13), custom_call_target="tpu_custom_call" | custom-call | tf_op jit(solution)/shard_map/factor_solve/pallas_call | solution.py:385
  (2 shorter events, 0.0 us)
Async XLA Ops:
  12.1 17.0 %collective-permute-start = (f32[3,128,512]{2,1,0:T(8,128)}, f32[3,128,512]{2,1,0:T(8,128)S(1)}, u32[]{:S(2)}, u32[]{:S(2)}) collective-permute-start(f32[3,128,512]{2,1,0:T(8,128)} %get-tuple-element.6), channel_id=1, source_target_pairs={{0,1},{1,2},{2,3},{3,0},{4,5},{5,6},{6,7},{7,4},{8,9},{9,10},{10,1... | collective-permute-start | bytes 2359304 | tf_op jit(solution)/shard_map/ppermute | solution.py:399
  13.8 16.5 %collective-permute-start.1 = (f32[3,128,512]{2,1,0:T(8,128)}, f32[3,128,512]{2,1,0:T(8,128)S(1)}, u32[]{:S(2)}, u32[]{:S(2)}) collective-permute-start(f32[3,128,512]{2,1,0:T(8,128)} %get-tuple-element.7), channel_id=1, source_target_pairs={{0,3},{1,0},{2,1},{3,2},{4,7},{5,4},{6,5},{7,6},{8,11},{9,8},{10,9... | collective-permute-start | bytes 2359304 | tf_op jit(solution)/shard_map/ppermute | solution.py:399
  29.1 1.2 copy-start
  30.3 0.9 copy-start.1

commit v4 on v3

--- a/solution.py
+++ b/solution.py
@@ -9,13 +9,14 @@
 GROUP = 4
 TURN = 3
 RING = 12
-
-def sparse_kernel(base, plan_ref, span_ref, tiles, panels, *rest):
+SPANS = 7 * 128
+
+def sparse_kernel(base, stage, plan_ref, tiles, panels, *rest):
     nout = len(rest) - 6
     outs = rest[:nout]
     lhs, rhs, sums, tsem, psem, osem = rest[nout:]
-    first = span_ref[0]
-    last = span_ref[1]
+    first = plan_ref[SPANS + stage]
+    last = plan_ref[SPANS + stage + 1]
     size = tiles.shape[1]
     rows_each = outs[0].shape[0]
     spare = nout * rows_each
@@ -83,55 +84,77 @@
     for c in copies:
         c.wait()
 
-def sparse_sum(plan, span, tiles, panels, base, shape):
+def sparse_sum(plan, stage, tiles, panels, base, shape):
     nout, rows = shape
     width = panels.shape[2]
     size = tiles.shape[1]
     return pl.pallas_call(
-        functools.partial(sparse_kernel, base),
+        functools.partial(sparse_kernel, base, stage),
         grid_spec=pltpu.PrefetchScalarGridSpec(
-            num_scalar_prefetch=2, grid=(),
+            num_scalar_prefetch=1, grid=(),
             in_specs=[pl.BlockSpec(memory_space=pl.ANY)] * 2,
             out_specs=[pl.BlockSpec(memory_space=pl.ANY)] * nout,
             scratch_shapes=[pltpu.VMEM((RING, size, GROUP * size), tiles.dtype), pltpu.VMEM((RING, GROUP * size, width), panels.dtype),
                             pltpu.VMEM((nout * rows + 1, size, width), jnp.float32),
                             pltpu.SemaphoreType.DMA((RING, GROUP)), pltpu.SemaphoreType.DMA((RING, GROUP)), pltpu.SemaphoreType.DMA((nout,))]),
         out_shape=[jax.ShapeDtypeStruct((rows, size, width), jnp.float32)] * nout,
-        compiler_params=pltpu.CompilerParams(vmem_limit_bytes=60 << 20),
+        compiler_params=pltpu.CompilerParams(vmem_limit_bytes=67_000_000),
         cost_estimate=pl.CostEstimate(flops=2 * 360 * 128 * 128 * 512 * rows * nout // 24, bytes_accessed=50_000_000 * rows * nout // 24, transcendentals=0),
         name="tile_sums",
-    )(plan, span, tiles, panels)
-
-def make_plan(places, count, me, ncol, chunk_rows):
-    rows = places[0]
-    cols = places[1]
-    n = rows.shape[0]
-    nplace = ncol * chunk_rows
-    ids = jnp.arange(n, dtype=jnp.int32)
-    half = chunk_rows // 2
-    dest = rows // chunk_rows
-    sub = rows % chunk_rows
-    step = jnp.where(sub < half, (me - 1 - dest) % ncol, (dest - 1 - me) % ncol)
-    live = ids < count
-    place = jnp.where(live, step * chunk_rows + sub, nplace)
-    rank = jnp.sum(((place[None, :] == place[:, None]) & (ids[None, :] < ids[:, None])).astype(jnp.int32), axis=1)
-    which = jnp.arange(nplace, dtype=jnp.int32)
-    held = jnp.sum((place[None, :] == which[:, None]).astype(jnp.int32), axis=1)
-    groups = (held + GROUP - 1) // GROUP
-    ahead = jnp.sum(jnp.where(which[None, :] < place[:, None], groups[None, :], 0), axis=1)
-    spot = jnp.where(live, ahead * GROUP + rank, -1)
-    word = ids | (cols << 9) | (place << 18) | (1 << 23)
-    total = -(-(n // GROUP + nplace) * GROUP // 128) * 128
-    plan = jnp.sum(jnp.where(spot[None, :] == jnp.arange(total, dtype=jnp.int32)[:, None], word[None, :], 0), axis=1)
-    n0 = jnp.sum(jnp.where(which < chunk_rows, groups, 0))
-    n1 = jnp.sum(groups)
-    return plan, jnp.stack([jnp.int32(0), n0]), jnp.stack([n0, n1])
-
+    )(plan, tiles, panels)
 
 HI = lax.Precision.HIGHEST
 
 def dot_hi(a, b, dims):
     return lax.dot_general(a, b, (dims, ((), ())), precision=HI, preferred_element_type=jnp.float32)
+
+def plan_kernel(ncol, chunk, count_ref, places_ref, plan_ref, wide):
+    me = lax.axis_index("col")
+    width = wide.shape[1]
+    wide[...] = jnp.zeros_like(wide)
+    wide[:, :places_ref.shape[1]] = places_ref[...]
+    rows = wide[0:1, :]
+    cols = wide[1:2, :]
+    ids = lax.broadcasted_iota(jnp.int32, (1, width), 1)
+    live = ids < count_ref[0, 0]
+    dest = jnp.zeros_like(rows)
+    for q in range(1, ncol):
+        dest = dest + (rows >= q * chunk).astype(jnp.int32)
+    sub = rows - dest * chunk
+    step = jnp.where(sub < chunk // 2, (me + 2 * ncol - 1 - dest) & (ncol - 1), (dest + 2 * ncol - 1 - me) & (ncol - 1))
+    place = step * chunk + sub
+    shelf = lax.broadcasted_iota(jnp.int32, (32, width), 0)
+    held = jnp.where(shelf == jnp.where(live, place, 99), 1.0, 0.0)
+    before = lax.broadcasted_iota(jnp.int32, (width, width), 0) < lax.broadcasted_iota(jnp.int32, (width, width), 1)
+    rank = jnp.dot(held.astype(jnp.bfloat16), jnp.where(before, 1.0, 0.0).astype(jnp.bfloat16), preferred_element_type=jnp.float32)
+    groups = (jnp.sum(held, axis=1, keepdims=True).astype(jnp.int32) + GROUP - 1) // GROUP
+    wide_groups = jnp.broadcast_to(groups.astype(jnp.float32), (32, 128))
+    under = lax.broadcasted_iota(jnp.int32, (32, 32), 1) < lax.broadcasted_iota(jnp.int32, (32, 32), 0)
+    ahead = jnp.dot(jnp.where(under, 1.0, 0.0).astype(jnp.bfloat16), wide_groups.astype(jnp.bfloat16), preferred_element_type=jnp.float32)
+    spot = jnp.sum(held * (rank + GROUP * ahead[:, 0:1]), axis=0, keepdims=True).astype(jnp.int32)
+    spot = jnp.where(live, spot, -1)
+    word = (ids + cols * 512 + place * (1 << 18) + (1 << 23)).astype(jnp.float32)
+    high = jnp.where(lax.broadcasted_iota(jnp.int32, (8, width), 0) == (spot >> 7), word, 0.0)
+    low = jnp.where(lax.broadcasted_iota(jnp.int32, (128, width), 0) == (spot & 127), 1.0, 0.0)
+    plan = dot_hi(high, low, ((1,), (1,))).astype(jnp.int32)
+    r8 = lax.broadcasted_iota(jnp.int32, (8, 128), 0)
+    c8 = lax.broadcasted_iota(jnp.int32, (8, 128), 1)
+    shelf8 = lax.broadcasted_iota(jnp.int32, (32, 128), 0)
+    n0 = jnp.sum(jnp.where(shelf8 < chunk, wide_groups, 0.0), axis=0, keepdims=True).astype(jnp.int32)
+    n1 = jnp.sum(wide_groups, axis=0, keepdims=True).astype(jnp.int32)
+    plan_ref[...] = jnp.where(r8 == 7, jnp.where(c8 == 1, n0, jnp.where(c8 == 2, n1, 0)), plan)
+
+def make_plan(places, count, ncol, chunk_rows):
+    width = -(-places.shape[1] // 128) * 128
+    return pl.pallas_call(
+        functools.partial(plan_kernel, ncol, chunk_rows),
+        out_shape=jax.ShapeDtypeStruct((8, 128), jnp.int32),
+        in_specs=[pl.BlockSpec(memory_space=pltpu.SMEM), pl.BlockSpec(memory_space=pltpu.VMEM)],
+        out_specs=pl.BlockSpec(memory_space=pltpu.VMEM),
+        scratch_shapes=[pltpu.VMEM((2, width), jnp.int32)],
+        name="tile_plan",
+    )(count, places).reshape(8 * 128)
+
 
 MESH = pl.DeviceIdType.MESH
 BLOCKS = (((0, 0), (2, 2), (0, 1), (2, 3), (0, 2)), ((1, 1), (3, 3), (1, 2), (0, 3), (1, 3)))
@@ -306,7 +329,7 @@
                         sem((2, count)), sem((3, 2, count)), sem((2, count)), sem((2, count)), sem((2, count)), sem((2, count)),
                         sem, sem, sem((pieces - 1,)), sem((pieces - 1,)), sem((zn - 1,)), sem((zn - 1,)),
                         sem((pieces - 1,)), sem((pieces - 1,)), sem((pieces,)), sem((pieces,))],
-        compiler_params=pltpu.CompilerParams(collective_id=0, has_side_effects=True, vmem_limit_bytes=60 << 20),
+        compiler_params=pltpu.CompilerParams(collective_id=0, has_side_effects=True, vmem_limit_bytes=67_000_000),
         name="ring_sum",
     )(up, down, later)
 
@@ -409,10 +432,9 @@
     chunk_rows = local_rows // tile_size
     half = chunk_rows // 2
     panels = sketch.reshape(-1, tile_size, sketch_width)
-    me = lax.axis_index("col")
-    plan, span0, span1 = make_plan(tile_places[0, 0], tile_counts[0, 0], me, col_devices, chunk_rows)
-    up, down = sparse_sum(plan, span0, tile_stack, panels, 0, (2, half))
-    (later,) = sparse_sum(plan, span1, tile_stack, panels, chunk_rows, (1, chunk_rows * (col_devices - 1)))
+    plan = make_plan(tile_places[0, 0], tile_counts, col_devices, chunk_rows)
+    up, down = sparse_sum(plan, 0, tile_stack, panels, 0, (2, half))
+    (later,) = sparse_sum(plan, 1, tile_stack, panels, chunk_rows, (1, chunk_rows * (col_devices - 1)))
     own, gram = ring_sum(shifted(up, 1), shifted(down, -1), later, (row_devices // 8, 4, col_devices))
     own_rows = own.reshape(local_rows, sketch_width)
     gram_blocks = gram.reshape(2, 5, 128, 128)

time: 135 us -> 129 us (0.956)
  other arithmetic: 6.48 us -> 0 us
  waiting for transfers between devices: 1.2 us -> 4.69 us
  Pallas kernels: 122 us -> 119 us
    ppermute x2, waiting for transfers between devices: 1.2 us -> 4.69 us  [shifted(): lax.ppermute(block, 'col', [(i, (i + distance) % count) for i in range(co...]
    another operation x2 -> x0, other arithmetic: 3.06 us -> none  [make_plan(): return (plan, jnp.stack([jnp.int32(0), n0]), jnp.stack([n0, n1]))]
    pallas_call x1, Pallas kernels: 78.7 us -> 76.6 us  [ring_sum(): pl.pallas_call(functools.partial(ring_kernel, dims), out_shape=(jax.Shape...]
    reduce_sum x5 -> x0, other arithmetic: 1.9 us -> none  [the longest x1 0.74 us: make_plan(): jnp.sum(jnp.where(spot[None, :] == jnp.arange(total, dtype=jnp.int32)[:,...]
    pallas_call x2 -> x3, Pallas kernels: 18.5 us -> 17.9 us  [the longest x2 15.9 us: sparse_sum(): pl.pallas_call(functools.partial(sparse_kernel, base, stage), grid_spec=p...]
  transfers between devices with their start and end apart: 2 -> 2, of which waited for: 1 -> 2; matrix products, arithmetic and copies ran while one was open for 1% -> 0% of each run, Pallas kernels for 9% -> 8%
where the time goes in v4:
time: 129 us
  Pallas kernels  119 us (92%)
  waiting for transfers between devices  4.69 us (4%)
  starting transfers between devices  4.03 us (3%)
  between operations  1.3 us (1%)
    pallas_call x1, Pallas kernels, ring_sum(): pl.pallas_call(functools.partial(ring_kernel, dims), out_shape=(jax.Shape...  76.6 us
    pallas_call x1, Pallas kernels, chol_solve(): pl.pallas_call(functools.partial(chol_kernel, scale), out_shape=(jax.Shap...  25 us
    pallas_call x2, Pallas kernels, sparse_sum(): pl.pallas_call(functools.partial(sparse_kernel, base, stage), grid_spec=p...  15.9 us
    ppermute x2, waiting for transfers between devices, shifted(): lax.ppermute(block, 'col', [(i, (i + distance) % count) for i in range(co...  4.69 us
    ppermute x2, starting transfers between devices, shifted(): lax.ppermute(block, 'col', [(i, (i + distance) % count) for i in range(co...  4.03 us
  transfers between devices with their start and end apart: 2, of which 2 were waited for; matrix products, arithmetic and copies ran while one was open for 0% of the time, Pallas kernels for 8%

profile of v4, /device:TPU:1, one launch (start us, length us, event | category | flops | bytes accessed | tf_op | source)
XLA Modules:
  0.0 129.4 jit_solution(658865553589933919)
XLA Ops:
  1.3 1.9 %tile_plan.1 = s32[8,128]{1,0:T(8,128)} custom-call(s32[1,1]{1,0:T(1,128)S(6)} %copy.6.count_ref, s32[2,360]{1,0:T(2,128)} %bitcast.14), custom_call_target="tpu_custom_call" | custom-call | tf_op jit(solution)/shard_map/tile_plan/pallas_call | solution.py:149
  3.2 5.7 %tile_sums.2 = (f32[3,128,512]{2,1,0:T(8,128)}, f32[3,128,512]{2,1,0:T(8,128)}) custom-call(s32[1024]{0:T(1024)} %bitcast.12, bf16[360,128,128]{2,1,0:T(8,128)(2,1)} %bitcast.8, bf16[384,128,512]{2,1,0:T(8,128)(2,1)} %bitcast.6), custom_call_target="tpu_custom_call" | custom-call | flops 1509949440 | bytes 12500000 | tf_op jit(solution)/shard_map/tile_sums/pallas_call | solution.py:91
  8.9 2.7 %collective-permute-start = (f32[3,128,512]{2,1,0:T(8,128)}, f32[3,128,512]{2,1,0:T(8,128)}, u32[]{:S(2)}, u32[]{:S(2)}) collective-permute-start(f32[3,128,512]{2,1,0:T(8,128)} %get-tuple-element.6), channel_id=1, source_target_pairs={{0,1},{1,2},{2,3},{3,0},{4,5},{5,6},{6,7},{7,4},{8,9},{9,10},{10,1... | collective-permute-start | bytes 2359304 | tf_op jit(solution)/shard_map/ppermute | solution.py:422
  11.6 1.3 %collective-permute-start.1 = (f32[3,128,512]{2,1,0:T(8,128)}, f32[3,128,512]{2,1,0:T(8,128)}, u32[]{:S(2)}, u32[]{:S(2)}) collective-permute-start(f32[3,128,512]{2,1,0:T(8,128)} %get-tuple-element.7), channel_id=1, source_target_pairs={{0,3},{1,0},{2,1},{3,2},{4,7},{5,4},{6,5},{7,6},{8,11},{9,8},{10,9... | collective-permute-start | bytes 2359304 | tf_op jit(solution)/shard_map/ppermute | solution.py:422
  12.9 10.2 %tile_sums.3.later_ref = f32[18,128,512]{2,1,0:T(8,128)} custom-call(s32[1024]{0:T(1024)} %bitcast.13, bf16[360,128,128]{2,1,0:T(8,128)(2,1)} %bitcast.9, bf16[384,128,512]{2,1,0:T(8,128)(2,1)} %bitcast.7), custom_call_target="tpu_custom_call" | custom-call | flops 4529848320 | bytes 37500000 | tf_op jit(solution)/shard_map/tile_sums/pallas_call | solution.py:91
  23.2 3.0 %collective-permute-done.up_ref = f32[3,128,512]{2,1,0:T(8,128)} collective-permute-done((f32[3,128,512]{2,1,0:T(8,128)}, f32[3,128,512]{2,1,0:T(8,128)}, u32[]{:S(2)}, u32[]{:S(2)}) %collective-permute-start) | collective-permute-done | bytes 786464 | tf_op jit(solution)/shard_map/ppermute | solution.py:422
  26.2 1.7 %collective-permute-done.1.down_ref = f32[3,128,512]{2,1,0:T(8,128)} collective-permute-done((f32[3,128,512]{2,1,0:T(8,128)}, f32[3,128,512]{2,1,0:T(8,128)}, u32[]{:S(2)}, u32[]{:S(2)}) %collective-permute-start.1) | collective-permute-done | bytes 786464 | tf_op jit(solution)/shard_map/ppermute | solution.py:422
  27.9 76.6 %ring_sum.1 = (f32[2,3,128,512]{3,2,1,0:T(8,128)}, f32[2,16,40,128]{3,2,1,0:T(8,128)}) custom-call(f32[3,128,512]{2,1,0:T(8,128)} %collective-permute-done.up_ref, f32[3,128,512]{2,1,0:T(8,128)} %collective-permute-done.1.down_ref, f32[18,128,512]{2,1,0:T(8,128)} %tile_sums.3.later_ref), custom_call_target="tpu_custom_call" | custom-call | tf_op jit(solution)/shard_map/ring_sum/pallas_call | solution.py:319
  104.4 25.0 %factor_solve.1 = (f32[768,512]{1,0:T(8,128)}, f32[512,512]{1,0:T(8,128)}) custom-call(f32[2,5,128,128]{3,2,1,0:T(8,128)} %bitcast.11, f32[768,512]{1,0:T(8,128)} %bitcast.10), custom_call_target="tpu_custom_call" | custom-call | tf_op jit(solution)/shard_map/factor_solve/pallas_call | solution.py:408
Async XLA Ops:
  8.9 17.3 %collective-permute-start = (f32[3,128,512]{2,1,0:T(8,128)}, f32[3,128,512]{2,1,0:T(8,128)}, u32[]{:S(2)}, u32[]{:S(2)}) collective-permute-start(f32[3,128,512]{2,1,0:T(8,128)} %get-tuple-element.6), channel_id=1, source_target_pairs={{0,1},{1,2},{2,3},{3,0},{4,5},{5,6},{6,7},{7,4},{8,9},{9,10},{10,1... | collective-permute-start | bytes 2359304 | tf_op jit(solution)/shard_map/ppermute | solution.py:422
  11.6 16.3 %collective-permute-start.1 = (f32[3,128,512]{2,1,0:T(8,128)}, f32[3,128,512]{2,1,0:T(8,128)}, u32[]{:S(2)}, u32[]{:S(2)}) collective-permute-start(f32[3,128,512]{2,1,0:T(8,128)} %get-tuple-element.7), channel_id=1, source_target_pairs={{0,3},{1,0},{2,1},{3,2},{4,7},{5,4},{6,5},{7,6},{8,11},{9,8},{10,9... | collective-permute-start | bytes 2359304 | tf_op jit(solution)/shard_map/ppermute | solution.py:422

commit v5 on v4

--- a/solution.py
+++ b/solution.py
@@ -54,7 +54,20 @@
 
     lax.fori_loop(0, sums.shape[0], clear, 0)
 
-    def step(turn, carry):
+    def leave(p):
+        for i, o in enumerate(outs):
+            @pl.when(lax.div(p, rows_each) == i)
+            def _():
+                pltpu.make_async_copy(sums.at[p], o.at[p - i * rows_each], osem.at[p]).start()
+
+    def leave_all(p, c):
+        leave(p)
+        return c
+
+    def place_of(g):
+        return ((plan_ref[jnp.minimum(g, last - 1) * GROUP] >> 18) & 31) - base
+
+    def step(turn, done):
         g0 = first + turn * TURN
         for u in range(TURN):
             g = g0 + u
@@ -69,20 +82,25 @@
                     def _():
                         tile.wait()
                         panel.wait()
+        ready = place_of(g0)
+        lax.fori_loop(done, ready, leave_all, 0)
         for u in range(TURN):
             g = g0 + u
             s = lax.rem(g, RING)
-            place = jnp.where(g < last, ((plan_ref[jnp.minimum(g, last - 1) * GROUP] >> 18) & 31) - base, spare)
+            place = jnp.where(g < last, place_of(g), spare)
             prod = jnp.dot(lhs[s], rhs[s], preferred_element_type=jnp.float32)
             sums[place] = sums[place] + prod
-        return carry
-
-    lax.fori_loop(0, lax.div(last - first + TURN - 1, TURN), step, 0)
-    copies = [pltpu.make_async_copy(sums.at[pl.ds(i * rows_each, rows_each)], o, osem.at[i]) for i, o in enumerate(outs)]
-    for c in copies:
-        c.start()
-    for c in copies:
-        c.wait()
+        return ready
+
+    done = lax.fori_loop(0, lax.div(last - first + TURN - 1, TURN), step, jnp.int32(0))
+    lax.fori_loop(done, spare, leave_all, 0)
+
+    def arrive(p, c):
+        pltpu.make_async_copy(sums.at[p], outs[0].at[0], osem.at[p]).wait()
+        return c
+
+    lax.fori_loop(0, spare, arrive, 0)
+
 
 def sparse_sum(plan, stage, tiles, panels, base, shape):
     nout, rows = shape
@@ -96,7 +114,7 @@
             out_specs=[pl.BlockSpec(memory_space=pl.ANY)] * nout,
             scratch_shapes=[pltpu.VMEM((RING, size, GROUP * size), tiles.dtype), pltpu.VMEM((RING, GROUP * size, width), panels.dtype),
                             pltpu.VMEM((nout * rows + 1, size, width), jnp.float32),
-                            pltpu.SemaphoreType.DMA((RING, GROUP)), pltpu.SemaphoreType.DMA((RING, GROUP)), pltpu.SemaphoreType.DMA((nout,))]),
+                            pltpu.SemaphoreType.DMA((RING, GROUP)), pltpu.SemaphoreType.DMA((RING, GROUP)), pltpu.SemaphoreType.DMA((nout * rows,))]),
         out_shape=[jax.ShapeDtypeStruct((rows, size, width), jnp.float32)] * nout,
         compiler_params=pltpu.CompilerParams(vmem_limit_bytes=67_000_000),
         cost_estimate=pl.CostEstimate(flops=2 * 360 * 128 * 128 * 512 * rows * nout // 24, bytes_accessed=50_000_000 * rows * nout // 24, transcendentals=0),
@@ -334,7 +352,7 @@
     )(up, down, later)
 
 
-def factor_block(a_ref, w_ref, u_ref):
+def factor_block(a_ref, w_ref, u_ref, c_ref):
     n = 128
     nv = n // 8
     lane = lax.broadcasted_iota(jnp.int32, (8, n), 1)
@@ -346,12 +364,16 @@
         for v in range(r, nv):
             for k in range(8):
                 col[k, v] = jnp.broadcast_to(a[v][:, 8 * r + k:8 * r + k + 1], (8, n))
+        for k in range(8):
+            c_ref[r, 8 * k:8 * k + 8, :] = col[k, r]
         e = {}
         for k in range(8):
             for j in range(k, 8):
-                e[k, j] = jnp.broadcast_to(col[j, r][k:k + 1, :], (8, n))
-        ra = [jnp.broadcast_to(a[r][k:k + 1, :], (8, n)) for k in range(8)]
-        rb = [jnp.broadcast_to(b[r][k:k + 1, :], (8, n)) for k in range(8)]
+                e[k, j] = c_ref[r, pl.ds(8 * j + k, 8, stride=0), :]
+        c_ref[r, 64:72, :] = a[r]
+        c_ref[r, 72:80, :] = b[r]
+        ra = [c_ref[r, pl.ds(64 + k, 8, stride=0), :] for k in range(8)]
+        rb = [c_ref[r, pl.ds(72 + k, 8, stride=0), :] for k in range(8)]
         for k in range(8):
             rs = lax.rsqrt(e[k, k])
             for j in range(k + 1, 8):
@@ -377,7 +399,7 @@
         u_ref[8 * r:8 * r + 8, :] = jnp.where(lane >= sub + 8 * r, ua, 0.0)
         w_ref[8 * r:8 * r + 8, :] = ub
 
-def chol_kernel(scale, g_ref, s_ref, x_ref, t_ref, gw, xs, d_ref, w_ref, u_ref):
+def chol_kernel(scale, g_ref, s_ref, x_ref, t_ref, gw, xs, d_ref, w_ref, u_ref, c_ref):
     n = gw.shape[0]
     nb = n // 128
     for h in range(2):
@@ -389,7 +411,7 @@
         lo = 128 * k
         hi = lo + 128
         d_ref[...] = gw[lo:hi, lo:hi]
-        factor_block(d_ref, w_ref, u_ref)
+        factor_block(d_ref, w_ref, u_ref, c_ref)
         w = w_ref[...]
         t_ref[lo:hi, lo:hi] = u_ref[...] * (1.0 / scale)
         if hi < n:
@@ -412,7 +434,7 @@
         out_specs=(pl.BlockSpec(memory_space=pltpu.VMEM),) * 2,
         scratch_shapes=[pltpu.VMEM((n, n), jnp.float32), pltpu.VMEM((m, n), jnp.float32),
                         pltpu.VMEM((128, 128), jnp.float32), pltpu.VMEM((128, 128), jnp.float32),
-                        pltpu.VMEM((128, 128), jnp.float32)],
+                        pltpu.VMEM((128, 128), jnp.float32), pltpu.VMEM((16, 80, 128), jnp.float32)],
         name="factor_solve",
     )(gram, rows)
 

time: 129 us -> 124 us (0.961)
  Pallas kernels: 119 us -> 111 us
  waiting for transfers between devices: 4.69 us -> 7.39 us
    pallas_call x1, Pallas kernels: 25 us -> 19.4 us  [chol_solve(): pl.pallas_call(functools.partial(chol_kernel, scale), out_shape=(jax.Shap...]
    pallas_call x1, Pallas kernels: 76.6 us -> 72.2 us  [ring_sum(): pl.pallas_call(functools.partial(ring_kernel, dims), out_shape=(jax.Shape...]
    ppermute x2, waiting for transfers between devices: 4.69 us -> 7.39 us  [shifted(): lax.ppermute(block, 'col', [(i, (i + distance) % count) for i in range(co...]
    pallas_call x2, Pallas kernels: 15.9 us -> 17.4 us  [sparse_sum(): pl.pallas_call(functools.partial(sparse_kernel, base, stage), grid_spec=p...]
  transfers between devices with their start and end apart: 2 -> 2, of which waited for: 2 -> 2; matrix products, arithmetic and copies ran while one was open for 0% -> 0% of each run, Pallas kernels for 8% -> 9%
where the time goes in v5:
time: 124 us
  Pallas kernels  111 us (90%)
  waiting for transfers between devices  7.39 us (6%)
  starting transfers between devices  4.21 us (3%)
  between operations  1.3 us (1%)
    pallas_call x1, Pallas kernels, ring_sum(): pl.pallas_call(functools.partial(ring_kernel, dims), out_shape=(jax.Shape...  72.2 us
    pallas_call x1, Pallas kernels, chol_solve(): pl.pallas_call(functools.partial(chol_kernel, scale), out_shape=(jax.Shap...  19.4 us
    pallas_call x2, Pallas kernels, sparse_sum(): pl.pallas_call(functools.partial(sparse_kernel, base, stage), grid_spec=p...  17.4 us
    ppermute x2, waiting for transfers between devices, shifted(): lax.ppermute(block, 'col', [(i, (i + distance) % count) for i in range(co...  7.39 us
    ppermute x2, starting transfers between devices, shifted(): lax.ppermute(block, 'col', [(i, (i + distance) % count) for i in range(co...  4.21 us
  transfers between devices with their start and end apart: 2, of which 2 were waited for; matrix products, arithmetic and copies ran while one was open for 0% of the time, Pallas kernels for 9%

profile of v5, /device:TPU:1, one launch (start us, length us, event | category | flops | bytes accessed | tf_op | source)
XLA Modules:
  0.0 123.8 jit_solution(1625134300673390274)
XLA Ops:
  1.3 1.9 %tile_plan.1 = s32[8,128]{1,0:T(8,128)} custom-call(s32[1,1]{1,0:T(1,128)S(6)} %copy.6.count_ref, s32[2,360]{1,0:T(2,128)} %bitcast.14), custom_call_target="tpu_custom_call" | custom-call | tf_op jit(solution)/shard_map/tile_plan/pallas_call | solution.py:167
  3.2 6.3 %tile_sums.2 = (f32[3,128,512]{2,1,0:T(8,128)}, f32[3,128,512]{2,1,0:T(8,128)}) custom-call(s32[1024]{0:T(1024)} %bitcast.12, bf16[360,128,128]{2,1,0:T(8,128)(2,1)} %bitcast.8, bf16[384,128,512]{2,1,0:T(8,128)(2,1)} %bitcast.6), custom_call_target="tpu_custom_call" | custom-call | flops 1509949440 | bytes 12500000 | tf_op jit(solution)/shard_map/tile_sums/pallas_call | solution.py:109
  9.6 4.2 %collective-permute-start = (f32[3,128,512]{2,1,0:T(8,128)}, f32[3,128,512]{2,1,0:T(8,128)}, u32[]{:S(2)}, u32[]{:S(2)}) collective-permute-start(f32[3,128,512]{2,1,0:T(8,128)} %get-tuple-element.6), channel_id=1, source_target_pairs={{0,1},{1,2},{2,3},{3,0},{4,5},{5,6},{6,7},{7,4},{8,9},{9,10},{10,1... | collective-permute-start | bytes 2359304 | tf_op jit(solution)/shard_map/ppermute | solution.py:444
  13.8 0.0 collective-permute-start.1
  13.8 11.0 %tile_sums.3.later_ref = f32[18,128,512]{2,1,0:T(8,128)} custom-call(s32[1024]{0:T(1024)} %bitcast.13, bf16[360,128,128]{2,1,0:T(8,128)(2,1)} %bitcast.9, bf16[384,128,512]{2,1,0:T(8,128)(2,1)} %bitcast.7), custom_call_target="tpu_custom_call" | custom-call | flops 4529848320 | bytes 37500000 | tf_op jit(solution)/shard_map/tile_sums/pallas_call | solution.py:109
  24.8 5.7 %collective-permute-done.up_ref = f32[3,128,512]{2,1,0:T(8,128)} collective-permute-done((f32[3,128,512]{2,1,0:T(8,128)}, f32[3,128,512]{2,1,0:T(8,128)}, u32[]{:S(2)}, u32[]{:S(2)}) %collective-permute-start) | collective-permute-done | bytes 786464 | tf_op jit(solution)/shard_map/ppermute | solution.py:444
  30.5 1.7 %collective-permute-done.1.down_ref = f32[3,128,512]{2,1,0:T(8,128)} collective-permute-done((f32[3,128,512]{2,1,0:T(8,128)}, f32[3,128,512]{2,1,0:T(8,128)}, u32[]{:S(2)}, u32[]{:S(2)}) %collective-permute-start.1) | collective-permute-done | bytes 786464 | tf_op jit(solution)/shard_map/ppermute | solution.py:444
  32.2 72.2 %ring_sum.1 = (f32[2,3,128,512]{3,2,1,0:T(8,128)}, f32[2,16,40,128]{3,2,1,0:T(8,128)}) custom-call(f32[3,128,512]{2,1,0:T(8,128)} %collective-permute-done.up_ref, f32[3,128,512]{2,1,0:T(8,128)} %collective-permute-done.1.down_ref, f32[18,128,512]{2,1,0:T(8,128)} %tile_sums.3.later_ref), custom_call_target="tpu_custom_call" | custom-call | tf_op jit(solution)/shard_map/ring_sum/pallas_call | solution.py:337
  104.4 19.4 %factor_solve.1 = (f32[768,512]{1,0:T(8,128)}, f32[512,512]{1,0:T(8,128)}) custom-call(f32[2,5,128,128]{3,2,1,0:T(8,128)} %bitcast.11, f32[768,512]{1,0:T(8,128)} %bitcast.10), custom_call_target="tpu_custom_call" | custom-call | tf_op jit(solution)/shard_map/factor_solve/pallas_call | solution.py:430
Async XLA Ops:
  9.6 20.9 %collective-permute-start = (f32[3,128,512]{2,1,0:T(8,128)}, f32[3,128,512]{2,1,0:T(8,128)}, u32[]{:S(2)}, u32[]{:S(2)}) collective-permute-start(f32[3,128,512]{2,1,0:T(8,128)} %get-tuple-element.6), channel_id=1, source_target_pairs={{0,1},{1,2},{2,3},{3,0},{4,5},{5,6},{6,7},{7,4},{8,9},{9,10},{10,1... | collective-permute-start | bytes 2359304 | tf_op jit(solution)/shard_map/ppermute | solution.py:444
  13.8 18.4 %collective-permute-start.1 = (f32[3,128,512]{2,1,0:T(8,128)}, f32[3,128,512]{2,1,0:T(8,128)}, u32[]{:S(2)}, u32[]{:S(2)}) collective-permute-start(f32[3,128,512]{2,1,0:T(8,128)} %get-tuple-element.7), channel_id=1, source_target_pairs={{0,3},{1,0},{2,1},{3,2},{4,7},{5,4},{6,5},{7,6},{8,11},{9,8},{10,9... | collective-permute-start | bytes 2359304 | tf_op jit(solution)/shard_map/ppermute | solution.py:444

commit v6 on v5

--- a/solution.py
+++ b/solution.py
@@ -7,8 +7,8 @@
 from jax.sharding import PartitionSpec as P
 
 GROUP = 4
-TURN = 3
-RING = 12
+TURN = 6
+RING = 18
 SPANS = 7 * 128
 
 def sparse_kernel(base, stage, plan_ref, tiles, panels, *rest):
@@ -25,22 +25,50 @@
         word = plan_ref[g * GROUP + k]
         s = lax.rem(g, RING)
         live = word >= (1 << 23)
-        tile = pltpu.make_async_copy(tiles.at[word & 511], lhs.at[s, :, pl.ds(k * size, size)], tsem.at[s, k])
-        panel = pltpu.make_async_copy(panels.at[(word >> 9) & 511], rhs.at[s, pl.ds(k * size, size), :], psem.at[s, k])
+        tile = pltpu.make_async_copy(tiles.at[word & 511], lhs.at[s, :, pl.ds(k * size, size)], tsem.at[s])
+        panel = pltpu.make_async_copy(panels.at[(word >> 9) & 511], rhs.at[s, pl.ds(k * size, size), :], psem.at[s])
         return live, tile, panel, s
 
+    def is_full(g):
+        return plan_ref[g * GROUP + GROUP - 1] >= (1 << 23)
+
     def issue(g):
-        for k in range(GROUP):
-            live, tile, panel, s = parts(g, k)
-            @pl.when(live)
-            def _():
+        full = is_full(g)
+        @pl.when(full)
+        def _():
+            for k in range(GROUP):
+                live, tile, panel, s = parts(g, k)
+                panel.start()
                 tile.start()
-                panel.start()
-            if k:
-                @pl.when(jnp.logical_not(live))
+        @pl.when(jnp.logical_not(full))
+        def _():
+            for k in range(GROUP):
+                live, tile, panel, s = parts(g, k)
+                @pl.when(live)
                 def _():
-                    lhs[s, :, k * size:(k + 1) * size] = jnp.zeros((size, size), lhs.dtype)
-                    rhs[s, k * size:(k + 1) * size, :] = jnp.zeros((size, rhs.shape[2]), rhs.dtype)
+                    panel.start()
+                    tile.start()
+                if k:
+                    @pl.when(jnp.logical_not(live))
+                    def _():
+                        lhs[s, :, k * size:(k + 1) * size] = jnp.zeros((size, size), lhs.dtype)
+                        rhs[s, k * size:(k + 1) * size, :] = jnp.zeros((size, rhs.shape[2]), rhs.dtype)
+
+    def settle(g):
+        full = is_full(g)
+        @pl.when(full)
+        def _():
+            s = lax.rem(g, RING)
+            pltpu.make_async_copy(lhs.at[s], lhs.at[s], tsem.at[s]).wait()
+            pltpu.make_async_copy(rhs.at[s], rhs.at[s], psem.at[s]).wait()
+        @pl.when(jnp.logical_not(full))
+        def _():
+            for k in range(GROUP):
+                live, tile, panel, s = parts(g, k)
+                @pl.when(live)
+                def _():
+                    tile.wait()
+                    panel.wait()
 
     def prime(g, c):
         issue(g)
@@ -76,12 +104,7 @@
                 issue(g + RING - TURN)
             @pl.when(g < last)
             def _():
-                for k in range(GROUP):
-                    live, tile, panel, s = parts(g, k)
-                    @pl.when(live)
-                    def _():
-                        tile.wait()
-                        panel.wait()
+                settle(g)
         ready = place_of(g0)
         lax.fori_loop(done, ready, leave_all, 0)
         for u in range(TURN):
@@ -114,7 +137,7 @@
             out_specs=[pl.BlockSpec(memory_space=pl.ANY)] * nout,
             scratch_shapes=[pltpu.VMEM((RING, size, GROUP * size), tiles.dtype), pltpu.VMEM((RING, GROUP * size, width), panels.dtype),
                             pltpu.VMEM((nout * rows + 1, size, width), jnp.float32),
-                            pltpu.SemaphoreType.DMA((RING, GROUP)), pltpu.SemaphoreType.DMA((RING, GROUP)), pltpu.SemaphoreType.DMA((nout * rows,))]),
+                            pltpu.SemaphoreType.DMA((RING,)), pltpu.SemaphoreType.DMA((RING,)), pltpu.SemaphoreType.DMA((nout * rows,))]),
         out_shape=[jax.ShapeDtypeStruct((rows, size, width), jnp.float32)] * nout,
         compiler_params=pltpu.CompilerParams(vmem_limit_bytes=67_000_000),
         cost_estimate=pl.CostEstimate(flops=2 * 360 * 128 * 128 * 512 * rows * nout // 24, bytes_accessed=50_000_000 * rows * nout // 24, transcendentals=0),

time: 124 us -> 123 us (level)
  Pallas kernels: 111 us -> 119 us
  waiting for transfers between devices: 7.39 us -> 0.01 us
  starting transfers between devices: 4.21 us -> 2.75 us
    pallas_call x2, Pallas kernels: 17.4 us -> 26.8 us  [sparse_sum(): pl.pallas_call(functools.partial(sparse_kernel, base, stage), grid_spec=p...]
    ppermute x2, waiting for transfers between devices: 7.39 us -> 0.01 us  [shifted(): lax.ppermute(block, 'col', [(i, (i + distance) % count) for i in range(co...]
    ppermute x2, starting transfers between devices: 4.21 us -> 2.75 us  [shifted(): lax.ppermute(block, 'col', [(i, (i + distance) % count) for i in range(co...]
  transfers between devices with their start and end apart: 2 -> 2, of which waited for: 2 -> 0; matrix products, arithmetic and copies ran while one was open for 0% -> 0% of each run, Pallas kernels for 9% -> 15%
where the time goes in v6:
time: 123 us
  Pallas kernels  119 us (97%)
  starting transfers between devices  2.75 us (2%)
  between operations  1.33 us (1%)
    pallas_call x1, Pallas kernels, ring_sum(): pl.pallas_call(functools.partial(ring_kernel, dims), out_shape=(jax.Shape...  71 us
    pallas_call x2, Pallas kernels, sparse_sum(): pl.pallas_call(functools.partial(sparse_kernel, base, stage), grid_spec=p...  26.8 us
    pallas_call x1, Pallas kernels, chol_solve(): pl.pallas_call(functools.partial(chol_kernel, scale), out_shape=(jax.Shap...  19.4 us
    ppermute x2, starting transfers between devices, shifted(): lax.ppermute(block, 'col', [(i, (i + distance) % count) for i in range(co...  2.75 us
  transfers between devices with their start and end apart: 2, of which 0 were waited for; matrix products, arithmetic and copies ran while one was open for 0% of the time, Pallas kernels for 15%

profile of v6, /device:TPU:1, one launch (start us, length us, event | category | flops | bytes accessed | tf_op | source)
XLA Modules:
  0.0 123.2 jit_solution(13196774941090703107)
XLA Ops:
  1.3 1.9 %tile_plan.1 = s32[8,128]{1,0:T(8,128)} custom-call(s32[1,1]{1,0:T(1,128)S(6)} %copy.6.count_ref, s32[2,360]{1,0:T(2,128)} %bitcast.14), custom_call_target="tpu_custom_call" | custom-call | tf_op jit(solution)/shard_map/tile_plan/pallas_call | solution.py:190
  3.2 8.7 %tile_sums.2 = (f32[3,128,512]{2,1,0:T(8,128)}, f32[3,128,512]{2,1,0:T(8,128)}) custom-call(s32[1024]{0:T(1024)} %bitcast.12, bf16[360,128,128]{2,1,0:T(8,128)(2,1)} %bitcast.8, bf16[384,128,512]{2,1,0:T(8,128)(2,1)} %bitcast.6), custom_call_target="tpu_custom_call" | custom-call | flops 1509949440 | bytes 12500000 | tf_op jit(solution)/shard_map/tile_sums/pallas_call | solution.py:132
  11.9 0.1 collective-permute-start
  12.0 2.7 %collective-permute-start.1 = (f32[3,128,512]{2,1,0:T(8,128)}, f32[3,128,512]{2,1,0:T(8,128)}, u32[]{:S(2)}, u32[]{:S(2)}) collective-permute-start(f32[3,128,512]{2,1,0:T(8,128)} %get-tuple-element.7), channel_id=1, source_target_pairs={{0,3},{1,0},{2,1},{3,2},{4,7},{5,4},{6,5},{7,6},{8,11},{9,8},{10,9... | collective-permute-start | bytes 2359304 | tf_op jit(solution)/shard_map/ppermute | solution.py:467
  14.6 18.1 %tile_sums.3.later_ref = f32[18,128,512]{2,1,0:T(8,128)} custom-call(s32[1024]{0:T(1024)} %bitcast.13, bf16[360,128,128]{2,1,0:T(8,128)(2,1)} %bitcast.9, bf16[384,128,512]{2,1,0:T(8,128)(2,1)} %bitcast.7), custom_call_target="tpu_custom_call" | custom-call | flops 4529848320 | bytes 37500000 | tf_op jit(solution)/shard_map/tile_sums/pallas_call | solution.py:132
  32.8 0.0 collective-permute-done.up_ref
  32.8 0.0 collective-permute-done.1.down_ref
  32.8 71.0 %ring_sum.1 = (f32[2,3,128,512]{3,2,1,0:T(8,128)}, f32[2,16,40,128]{3,2,1,0:T(8,128)}) custom-call(f32[3,128,512]{2,1,0:T(8,128)} %collective-permute-done.up_ref, f32[3,128,512]{2,1,0:T(8,128)} %collective-permute-done.1.down_ref, f32[18,128,512]{2,1,0:T(8,128)} %tile_sums.3.later_ref), custom_call_target="tpu_custom_call" | custom-call | tf_op jit(solution)/shard_map/ring_sum/pallas_call | solution.py:360
  103.8 19.4 %factor_solve.1 = (f32[768,512]{1,0:T(8,128)}, f32[512,512]{1,0:T(8,128)}) custom-call(f32[2,5,128,128]{3,2,1,0:T(8,128)} %bitcast.11, f32[768,512]{1,0:T(8,128)} %bitcast.10), custom_call_target="tpu_custom_call" | custom-call | tf_op jit(solution)/shard_map/factor_solve/pallas_call | solution.py:453
Async XLA Ops:
  11.9 20.9 %collective-permute-start = (f32[3,128,512]{2,1,0:T(8,128)}, f32[3,128,512]{2,1,0:T(8,128)}, u32[]{:S(2)}, u32[]{:S(2)}) collective-permute-start(f32[3,128,512]{2,1,0:T(8,128)} %get-tuple-element.6), channel_id=1, source_target_pairs={{0,1},{1,2},{2,3},{3,0},{4,5},{5,6},{6,7},{7,4},{8,9},{9,10},{10,1... | collective-permute-start | bytes 2359304 | tf_op jit(solution)/shard_map/ppermute | solution.py:467
  12.0 20.8 %collective-permute-start.1 = (f32[3,128,512]{2,1,0:T(8,128)}, f32[3,128,512]{2,1,0:T(8,128)}, u32[]{:S(2)}, u32[]{:S(2)}) collective-permute-start(f32[3,128,512]{2,1,0:T(8,128)} %get-tuple-element.7), channel_id=1, source_target_pairs={{0,3},{1,0},{2,1},{3,2},{4,7},{5,4},{6,5},{7,6},{8,11},{9,8},{10,9... | collective-permute-start | bytes 2359304 | tf_op jit(solution)/shard_map/ppermute | solution.py:467

commit v7 on v6

--- a/solution.py
+++ b/solution.py
@@ -203,7 +203,7 @@
 
 def ring_kernel(dims, up_ref, down_ref, later_ref, rows_ref, out_ref,
                 head, later, box1, box2, part, mate, mine, inbox, tower, full,
-                hsem, lsem, s1, r1, s2, r2, cs, cr, ps, pr, zs, zr, gs, gr, fs, fr):
+                hsem, lsem, osem, s1, r1, s2, r2, cs, cr, ps, pr, zs, zr, gs, gr, fs, fr):
     zn, xn, yn = dims
     row = lax.axis_index("row")
     y = lax.axis_index("col")
@@ -244,6 +244,9 @@
         p = (2 * step + d) * count + i
         return pltpu.make_async_copy(later_ref.at[p], later.at[step, d, i], lsem.at[step, d, i])
 
+    def row_copy(i, d):
+        return pltpu.make_async_copy(box2.at[d, i], rows_ref.at[d, i], osem.at[d, i])
+
     def hop1(i, d):
         return remote(head.at[d, i], box1.at[d, i], s1.at[d, i], r1.at[d, i], ring[d])
 
@@ -286,7 +289,8 @@
             later_copy(2, i, d).wait()
             hop2(i, d).wait_recv()
             total = box2[d, i] + later[2, d, i]
-            rows_ref[d, i] = total
+            box2[d, i] = total
+            row_copy(i, d).start()
             for a in range(4):
                 got = dot_hi(total[:, 128 * a:128 * a + 128], total[:, 128 * a:], ((0,), (0,)))
                 for j in range(a, 4):
@@ -346,6 +350,7 @@
         for d in range(2):
             hop1(i, d).wait_send()
             hop2(i, d).wait_send()
+            row_copy(i, d).wait()
         return c
 
     lax.fori_loop(0, count, drain, 0)
@@ -361,13 +366,13 @@
         functools.partial(ring_kernel, dims),
         out_shape=(jax.ShapeDtypeStruct((2, count, tall, n), f32), jax.ShapeDtypeStruct((2, pieces, deep // pieces, 128), f32)),
         in_specs=[pl.BlockSpec(memory_space=pl.ANY)] * 3,
-        out_specs=(pl.BlockSpec(memory_space=pltpu.VMEM),) * 2,
+        out_specs=(pl.BlockSpec(memory_space=pl.ANY), pl.BlockSpec(memory_space=pltpu.VMEM)),
         scratch_shapes=[pltpu.VMEM((2, count, tall, n), f32), pltpu.VMEM((3, 2, count, tall, n), f32),
                         pltpu.VMEM((2, count, tall, n), f32), pltpu.VMEM((2, count, tall, n), f32),
                         pltpu.VMEM((2, deep, 128), f32), pltpu.VMEM((deep, 128), f32), pltpu.VMEM((deep, 128), f32),
                         pltpu.VMEM((pieces - 1, deep // pieces, 128), f32), pltpu.VMEM((zn, deep // pieces, 128), f32),
                         pltpu.VMEM((2, pieces, deep // pieces, 128), f32),
-                        sem((2, count)), sem((3, 2, count)), sem((2, count)), sem((2, count)), sem((2, count)), sem((2, count)),
+                        sem((2, count)), sem((3, 2, count)), sem((2, count)), sem((2, count)), sem((2, count)), sem((2, count)), sem((2, count)),
                         sem, sem, sem((pieces - 1,)), sem((pieces - 1,)), sem((zn - 1,)), sem((zn - 1,)),
                         sem((pieces - 1,)), sem((pieces - 1,)), sem((pieces,)), sem((pieces,))],
         compiler_params=pltpu.CompilerParams(collective_id=0, has_side_effects=True, vmem_limit_bytes=67_000_000),

time: 123 us -> 123 us (level)
  Pallas kernels: 119 us -> 117 us
  waiting for transfers between devices: 0.01 us -> 1.79 us
    pallas_call x2, Pallas kernels: 26.8 us -> 21.5 us  [sparse_sum(): pl.pallas_call(functools.partial(sparse_kernel, base, stage), grid_spec=p...]
    pallas_call x1, Pallas kernels: 71 us -> 74.2 us  [ring_sum(): pl.pallas_call(functools.partial(ring_kernel, dims), out_shape=(jax.Shape...]
    ppermute x2, waiting for transfers between devices: 0.01 us -> 1.79 us  [shifted(): lax.ppermute(block, 'col', [(i, (i + distance) % count) for i in range(co...]
  transfers between devices with their start and end apart: 2 -> 2, of which waited for: 0 -> 1; matrix products, arithmetic and copies ran while one was open for 0% -> 0% of each run, Pallas kernels for 15% -> 11%
where the time goes in v7:
time: 123 us
  Pallas kernels  117 us (95%)
  starting transfers between devices  2.75 us (2%)
  waiting for transfers between devices  1.79 us (1%)
  between operations  1.3 us (1%)
    pallas_call x1, Pallas kernels, ring_sum(): pl.pallas_call(functools.partial(ring_kernel, dims), out_shape=(jax.Shape...  74.2 us
    pallas_call x2, Pallas kernels, sparse_sum(): pl.pallas_call(functools.partial(sparse_kernel, base, stage), grid_spec=p...  21.5 us
    pallas_call x1, Pallas kernels, chol_solve(): pl.pallas_call(functools.partial(chol_kernel, scale), out_shape=(jax.Shap...  19.4 us
    ppermute x2, starting transfers between devices, shifted(): lax.ppermute(block, 'col', [(i, (i + distance) % count) for i in range(co...  2.75 us
  transfers between devices with their start and end apart: 2, of which 1 were waited for; matrix products, arithmetic and copies ran while one was open for 0% of the time, Pallas kernels for 11%

profile of v7, /device:TPU:1, one launch (start us, length us, event | category | flops | bytes accessed | tf_op | source)
XLA Modules:
  0.0 122.8 jit_solution(14113554464572115076)
XLA Ops:
  1.3 1.9 %tile_plan.1 = s32[8,128]{1,0:T(8,128)} custom-call(s32[1,1]{1,0:T(1,128)S(6)} %copy.6.count_ref, s32[2,360]{1,0:T(2,128)} %bitcast.14), custom_call_target="tpu_custom_call" | custom-call | tf_op jit(solution)/shard_map/tile_plan/pallas_call | solution.py:190
  3.2 7.5 %tile_sums.2 = (f32[3,128,512]{2,1,0:T(8,128)}, f32[3,128,512]{2,1,0:T(8,128)}) custom-call(s32[1024]{0:T(1024)} %bitcast.12, bf16[360,128,128]{2,1,0:T(8,128)(2,1)} %bitcast.8, bf16[384,128,512]{2,1,0:T(8,128)(2,1)} %bitcast.6), custom_call_target="tpu_custom_call" | custom-call | flops 1509949440 | bytes 12500000 | tf_op jit(solution)/shard_map/tile_sums/pallas_call | solution.py:132
  10.8 0.1 collective-permute-start
  10.9 2.6 %collective-permute-start.1 = (f32[3,128,512]{2,1,0:T(8,128)}, f32[3,128,512]{2,1,0:T(8,128)}, u32[]{:S(2)}, u32[]{:S(2)}) collective-permute-start(f32[3,128,512]{2,1,0:T(8,128)} %get-tuple-element.7), channel_id=1, source_target_pairs={{0,3},{1,0},{2,1},{3,2},{4,7},{5,4},{6,5},{7,6},{8,11},{9,8},{10,9... | collective-permute-start | bytes 2359304 | tf_op jit(solution)/shard_map/ppermute | solution.py:472
  13.5 13.9 %tile_sums.3.later_ref = f32[18,128,512]{2,1,0:T(8,128)} custom-call(s32[1024]{0:T(1024)} %bitcast.13, bf16[360,128,128]{2,1,0:T(8,128)(2,1)} %bitcast.9, bf16[384,128,512]{2,1,0:T(8,128)(2,1)} %bitcast.7), custom_call_target="tpu_custom_call" | custom-call | flops 4529848320 | bytes 37500000 | tf_op jit(solution)/shard_map/tile_sums/pallas_call | solution.py:132
  27.5 1.8 %collective-permute-done.up_ref = f32[3,128,512]{2,1,0:T(8,128)} collective-permute-done((f32[3,128,512]{2,1,0:T(8,128)}, f32[3,128,512]{2,1,0:T(8,128)}, u32[]{:S(2)}, u32[]{:S(2)}) %collective-permute-start) | collective-permute-done | bytes 786464 | tf_op jit(solution)/shard_map/ppermute | solution.py:472
  29.2 0.0 collective-permute-done.1.down_ref
  29.3 74.2 %ring_sum.1 = (f32[2,3,128,512]{3,2,1,0:T(8,128)}, f32[2,16,40,128]{3,2,1,0:T(8,128)}) custom-call(f32[3,128,512]{2,1,0:T(8,128)} %collective-permute-done.up_ref, f32[3,128,512]{2,1,0:T(8,128)} %collective-permute-done.1.down_ref, f32[18,128,512]{2,1,0:T(8,128)} %tile_sums.3.later_ref), custom_call_target="tpu_custom_call" | custom-call | tf_op jit(solution)/shard_map/ring_sum/pallas_call | solution.py:365
  103.5 19.4 %factor_solve.1 = (f32[768,512]{1,0:T(8,128)}, f32[512,512]{1,0:T(8,128)}) custom-call(f32[2,5,128,128]{3,2,1,0:T(8,128)} %bitcast.11, f32[768,512]{1,0:T(8,128)} %bitcast.10), custom_call_target="tpu_custom_call" | custom-call | tf_op jit(solution)/shard_map/factor_solve/pallas_call | solution.py:458
Async XLA Ops:
  10.8 18.5 %collective-permute-start = (f32[3,128,512]{2,1,0:T(8,128)}, f32[3,128,512]{2,1,0:T(8,128)}, u32[]{:S(2)}, u32[]{:S(2)}) collective-permute-start(f32[3,128,512]{2,1,0:T(8,128)} %get-tuple-element.6), channel_id=1, source_target_pairs={{0,1},{1,2},{2,3},{3,0},{4,5},{5,6},{6,7},{7,4},{8,9},{9,10},{10,1... | collective-permute-start | bytes 2359304 | tf_op jit(solution)/shard_map/ppermute | solution.py:472
  10.9 18.4 %collective-permute-start.1 = (f32[3,128,512]{2,1,0:T(8,128)}, f32[3,128,512]{2,1,0:T(8,128)}, u32[]{:S(2)}, u32[]{:S(2)}) collective-permute-start(f32[3,128,512]{2,1,0:T(8,128)} %get-tuple-element.7), channel_id=1, source_target_pairs={{0,3},{1,0},{2,1},{3,2},{4,7},{5,4},{6,5},{7,6},{8,11},{9,8},{10,9... | collective-permute-start | bytes 2359304 | tf_op jit(solution)/shard_map/ppermute | solution.py:472
